TPU v7x, 32 devices: a whole 2x2x4 slice. The times are simulated.
32 devices in a mesh: tensor: 4 (over x, core), section: 2 (over y), dp: 4 (over z).
Axes of the slice: x: 2, y: 2, z: 4, core: 2. Of those that a mesh axis runs over, the one named last changes fastest.
Arguments:
- block_input: bfloat16 [4096, 6144], P(('section', 'dp')), may hold values from -6 to 6
- output_gradient: bfloat16 [4096, 6144], P(('section', 'dp')), may hold values from -6 to 6
- queries: bfloat16 [4096, 3072], P(('section', 'dp'), 'tensor'), may hold values from -8 to 8
- saved_keys: bfloat16 [4096, 3072], P(('section', 'dp'), 'tensor'), may hold values from -8 to 8
- values: bfloat16 [4096, 3072], P(('section', 'dp'), 'tensor'), may hold values from -6 to 6
- document_index: int32 [4096], P(('section', 'dp')), may hold values from 0 to 4095, as said below
- output_weight: bfloat16 [6144, 3072], P(('section', 'dp'), 'tensor'), may hold values from -0.109375 to 0.109375
- adapter_down_weight: bfloat16 [2, 6144, 128], P('section'), may hold values from -0.078125 to 0.078125
- adapter_up_weight: bfloat16 [2, 128, 3072], P('section', None, 'tensor'), may hold values from -0.5 to 0.5
Outputs:
- grad_out: float32 [6144, 3072], P(('section', 'dp'), 'tensor')
- grad_value_proj: float32 [6144, 3072], P(('section', 'dp'), 'tensor')
- grad_query: bfloat16 [4096, 3072], P(('section', 'dp'), 'tensor')
- grad_key: bfloat16 [4096, 3072], P(('section', 'dp'), 'tensor')
- grad_down: float32 [2, 6144, 128], P('section', 'dp')
- grad_up: float32 [2, 128, 3072], P('section', 'dp', 'tensor')
Inputs may be any that keep to these rules, and one draw needn't show every extreme that they name: `document_index`: ids never fall along the tokens; a document's id is the index of its first token, each block of 512 tokens starts a new document, and the last token is a document of its own.
All inputs are finite; a program needn't handle non-finite values.
Results may differ from a plain program's by a relative error of at most 0.015.
Values may be sent and summed in bfloat16 or wider, within the bound.
A program may use at most 192 MiB of HBM per device.

v0:
```python
import jax
import jax.numpy as jnp
from jax import lax
from jax.sharding import PartitionSpec as P

HD = 128


def attend(queries, saved_keys, values, attn_grad, document_index):
    token_rows = queries.shape[0]
    head_count = queries.shape[1] // HD
    score_scale = HD ** (-0.5)
    query_heads = queries.reshape(token_rows, head_count, HD)
    key_heads = saved_keys.reshape(token_rows, head_count, HD)
    value_heads = values.reshape(token_rows, head_count, HD)
    grad_heads = attn_grad.reshape(token_rows, head_count, HD)
    scores = (
        jnp.einsum("qhd,khd->hqk", query_heads, key_heads, preferred_element_type=jnp.float32)
        * score_scale
    )
    position = jnp.arange(token_rows, dtype=jnp.int32)
    allowed = (document_index[:, None] == document_index[None, :]) & (
        position[None, :] <= position[:, None]
    )
    scores = jnp.where(allowed[None], scores, jnp.float32(-1e30))
    top_score = jnp.max(scores, axis=-1, keepdims=True)
    expo = jnp.exp(scores - top_score)
    attn_probs = expo / jnp.sum(expo, axis=-1, keepdims=True)
    probs_half = attn_probs.astype(jnp.bfloat16)
    output = jnp.einsum(
        "hqk,khd->qhd", probs_half, value_heads, preferred_element_type=jnp.float32
    ).astype(jnp.bfloat16)
    value_gradient = jnp.einsum(
        "hqk,qhd->khd", probs_half, grad_heads, preferred_element_type=jnp.float32
    ).astype(jnp.bfloat16)
    grad_prob = jnp.einsum(
        "qhd,khd->hqk", grad_heads, value_heads, preferred_element_type=jnp.float32
    )
    row_delta = jnp.sum(attn_probs * grad_prob, axis=-1, keepdims=True)
    grad_score = (attn_probs * (grad_prob - row_delta) * score_scale).astype(jnp.bfloat16)
    grad_query = jnp.einsum(
        "hqk,khd->qhd", grad_score, key_heads, preferred_element_type=jnp.float32
    ).astype(jnp.bfloat16)
    grad_key = jnp.einsum(
        "hqk,qhd->khd", grad_score, query_heads, preferred_element_type=jnp.float32
    ).astype(jnp.bfloat16)
    width = head_count * HD
    return (
        output.reshape(token_rows, width),
        value_gradient.reshape(token_rows, width),
        grad_query.reshape(token_rows, width),
        grad_key.reshape(token_rows, width),
    )


def local(
    block_input,
    output_gradient,
    queries,
    saved_keys,
    values,
    document_index,
    output_weight,
    adapter_down_weight,
    adapter_up_weight,
):
    token_rows = block_input.shape[0]
    local_width = queries.shape[1]
    contract_rows = (((0,), (0,)), ((), ()))
    grad_cols = output_gradient
    attn_grad = jnp.dot(
        grad_cols,
        lax.all_gather(output_weight, ("section", "dp"), axis=0, tiled=True),
        preferred_element_type=jnp.float32,
    ).astype(jnp.bfloat16)
    output, value_gradient, grad_query, grad_key = attend(
        queries, saved_keys, values, attn_grad, document_index
    )
    grad_cols = output_gradient
    out_term = lax.dot_general(grad_cols, output, contract_rows, preferred_element_type=jnp.float32)
    value_term = lax.dot_general(
        block_input, value_gradient, contract_rows, preferred_element_type=jnp.float32
    )
    summed = lax.psum_scatter(
        jnp.concatenate([out_term, value_term], axis=1).astype(jnp.bfloat16),
        ("section", "dp"),
        scatter_dimension=0,
        tiled=True,
    ).astype(jnp.float32)
    narrow_product = jnp.dot(
        block_input, adapter_down_weight[0], preferred_element_type=jnp.float32
    ).astype(jnp.bfloat16)
    mix_part = lax.dot_general(
        value_gradient,
        adapter_up_weight[0],
        (((1,), (1,)), ((), ())),
        preferred_element_type=jnp.float32,
    )
    mix_term = lax.psum(mix_part.astype(jnp.bfloat16), "tensor")
    down_part = lax.dot_general(
        block_input, mix_term, contract_rows, preferred_element_type=jnp.float32
    )
    up_part = lax.dot_general(
        narrow_product, value_gradient, contract_rows, preferred_element_type=jnp.float32
    )
    down_total, up_total = (
        lax.psum_scatter(
            down_part.astype(jnp.bfloat16), "dp", scatter_dimension=0, tiled=True
        ).astype(jnp.float32),
        lax.psum_scatter(
            up_part.astype(jnp.bfloat16), "dp", scatter_dimension=0, tiled=True
        ).astype(jnp.float32),
    )
    token_factor = (token_rows * lax.axis_size("section") * lax.axis_size("dp")) ** (-0.5)
    adapter_factor = (token_rows * lax.axis_size("dp")) ** (-0.5)
    grad_out = summed[:, :local_width] * token_factor
    grad_value_proj = summed[:, local_width:] * token_factor
    return (
        grad_out,
        grad_value_proj,
        grad_query,
        grad_key,
        (down_total * adapter_factor)[None],
        (up_total * adapter_factor)[None],
    )


def solution(mesh):
    return jax.shard_map(
        local,
        mesh=mesh,
        in_specs=(
            P(("section", "dp"), None),
            P(("section", "dp"), None),
            P(("section", "dp"), "tensor"),
            P(("section", "dp"), "tensor"),
            P(("section", "dp"), "tensor"),
            P(("section", "dp")),
            P(("section", "dp"), "tensor"),
            P("section", None, None),
            P("section", None, "tensor"),
        ),
        out_specs=(
            P(("section", "dp"), "tensor"),
            P(("section", "dp"), "tensor"),
            P(("section", "dp"), "tensor"),
            P(("section", "dp"), "tensor"),
            P("section", "dp", None),
            P("section", "dp", "tensor"),
        ),
        check_vma=False,
    )
```

profile of v0, /device:TPU:9, one launch (start us, length us, event | category | flops | bytes accessed | tf_op | source)
XLA Modules:
  0.0 586.9 jit_solution(15455212225179713954)
XLA Ops:
  7.2 0.0 copy-start
  7.2 0.0 all-gather.2.cloned.1.call-start
  7.2 0.7 all-gather.2.cloned.1.call-update
  7.9 0.0 all-reduce.2.cloned.1.call-start
  8.0 2.3 copy.32
  10.3 1.4 copy.33
  11.7 0.0 copy-start.2
  11.7 1.7 copy.36
  13.4 1.0 fusion.41
  14.3 6.5 %fusion.51 = (f32[6,512]{1,0:T(8,128)S(1)}, f32[6,512,512]{1,2,0:T(8,128)}) fusion(pred[512,512]{0,1:T(8,128)(4,1)S(1)} %fusion.41, bf16[512,6,128]{0,2,1:T(8,128)(2,1)} %bitcast.63, bf16[512,6,128]{0,2,1:T(8,128)(2,1)S(1)} %bitcast.61), kind=kOutput, calls=%fused_computation.49 | convolution fusion | flops 408945152 | bytes 8138752 | tf_op jit(solution)/shard_map/sub | solution.py:27
  20.8 0.0 copy-done.2
  20.8 4.6 fusion.24
  25.5 121.7 %all-gather.2.cloned.1.call-done = bf16[6144,768]{1,0:T(8,128)(2,1)} async-done(((bf16[768,768]{1,0:T(8,128)(2,1)}), bf16[6144,768]{1,0:T(8,128)(2,1)}) %all-gather.2.cloned.1.call-update) | async-done | bytes 9437200 | tf_op jit(solution)/shard_map/all_gather | solution.py:73
  147.1 10.6 %convolution_convert_fusion.3 = bf16[512,768]{1,0:T(8,128)(2,1)} fusion(bf16[512,6144]{1,0:T(8,128)(2,1)} %param.10, bf16[6144,768]{1,0:T(8,128)(2,1)} %all-gather.2.cloned.1.call-done), kind=kOutput, calls=%fused_computation.33 | convolution fusion | flops 4832231424 | bytes 16515072 | tf_op jit(solution)/shard_map/dot_general | solution.py:71
  157.7 1.4 copy.38
  159.2 0.0 copy-start.7
  159.2 4.0 fusion.27
  163.2 0.0 copy-start.5
  163.2 0.9 copy-done.5
  164.0 0.0 copy-done.7
  164.0 1.1 convolution_convert_fusion.5
  165.1 0.0 all-reduce.2.cloned.1.call-update
  165.1 0.0 reduce-scatter.8.cloned.1.call-start
  165.2 0.0 copy-done
  165.2 6.1 %convolution_convert_fusion.4 = bf16[128,768]{1,0:T(8,128)(2,1)} fusion(bf16[512,768]{0,1:T(8,128)(2,1)} %bitcast.68, bf16[512,6144]{1,0:T(8,128)(2,1)} %param.9, bf16[1,6144,128]{2,1,0:T(8,128)(2,1)S(1)} %copy-done), kind=kOutput, calls=%fused_computation.34 | convolution fusion | flops 906133504 | bytes 8847360 | tf_op jit(solution)/shard_map/dot_general | solution.py:103
  171.3 0.0 reduce-scatter.8.cloned.1.call-update
  171.3 0.0 copy-start.8
  171.3 0.0 reduce-scatter.6.cloned.1.call-start
  171.4 24.7 %all-reduce.2.cloned.1.call-done = bf16[512,128]{1,0:T(8,128)(2,1)} async-done(((bf16[512,128]{1,0:T(8,128)(2,1)}), bf16[512,128]{1,0:T(8,128)(2,1)}) %all-reduce.2.cloned.1.call-update) | async-done | bytes 131088 | tf_op jit(solution)/shard_map/psum | solution.py:99
  196.1 5.0 fusion.4
  201.1 0.0 reduce-scatter.6.cloned.1.call-update
  201.1 0.2 reduce-scatter.4.cloned.1.call-start
  201.4 0.0 copy-done.8
  201.4 0.0 copy-start.6
  201.4 8.1 %fusion.2 = bf16[6144,768]{0,1:T(8,128)(2,1)S(1)} fusion(bf16[512,768]{0,1:T(8,128)(2,1)S(1)} %bitcast.70, bf16[512,6144]{1,0:T(8,128)(2,1)} %param.10), kind=kOutput, calls=%fused_computation.5 | convolution fusion | flops 4836556800 | bytes 16515072 | tf_op jit(solution)/shard_map/dot_general | solution.py:80
  209.5 0.0 copy-done.6
  209.5 8.1 %fusion.3 = bf16[6144,768]{0,1:T(8,128)(2,1)S(1)} fusion(bf16[512,768]{0,1:T(8,128)(2,1)S(1)} %bitcast.69, bf16[512,6144]{1,0:T(8,128)(2,1)} %param.9), kind=kOutput, calls=%fused_computation.6 | convolution fusion | flops 4836556800 | bytes 16515072 | tf_op jit(solution)/shard_map/dot_general | solution.py:81
  217.6 21.3 %pad_maximum_fusion = bf16[6144,1536]{0,1:T(8,128)(2,1)} fusion(bf16[6144,768]{0,1:T(8,128)(2,1)S(1)} %fusion.3, bf16[6144,768]{0,1:T(8,128)(2,1)S(1)} %fusion.2), kind=kLoop, calls=%fused_computation.2 | loop fusion | flops 37748736 | bytes 37748736 | tf_op jit(solution)/shard_map/concatenate | solution.py:85
  238.9 0.0 reduce-scatter.4.cloned.1.call-update
  238.9 0.0 copy-start.4
  238.9 3.7 fusion.52
  242.6 0.0 copy-done.4
  242.6 0.0 copy-start.3
  242.6 9.9 %fusion.33 = bf16[6,512,128]{1,2,0:T(8,128)(2,1)S(1)} fusion(bf16[512,6,128]{0,2,1:T(8,128)(2,1)S(1)} %bitcast.64, f32[6,512,512]{1,2,0:T(8,128)} %fusion.52, f32[6,512,512]{1,2,0:T(8,128)} %get-tuple-element.21, f32[6,512]{1,0:T(8,128)S(1)} %get-tuple-element.20), kind=kOutput, calls=%fused_computation.32 | convolution fusion | flops 414060032 | bytes 14168064 | tf_op jit(solution)/shard_map/hqk,qhd->khd/dot_general | solution.py:44
  252.5 1.2 copy.47
  253.7 0.0 copy-done.3
  253.7 10.9 %fusion.30 = bf16[6,512,128]{1,2,0:T(8,128)(2,1)S(1)} fusion(bf16[512,6,128]{0,2,1:T(8,128)(2,1)S(1)} %bitcast.62, f32[6,512,512]{1,2,0:T(8,128)} %fusion.52, f32[6,512,512]{1,2,0:T(8,128)} %get-tuple-element.21, f32[6,512]{1,0:T(8,128)S(1)} %get-tuple-element.20), kind=kOutput, calls=%fused_computation.31 | convolution fusion | flops 414060032 | bytes 14168064 | tf_op jit(solution)/shard_map/hqk,khd->qhd/dot_general | solution.py:41
  264.6 1.2 copy.46
  265.8 0.0 reduce-scatter.8.cloned.1.call-done
  265.8 1.5 multiply_bitcast_fusion.1
  267.2 0.0 reduce-scatter.6.cloned.1.call-done
  267.2 1.1 multiply_bitcast_fusion
  268.3 1.1 copy.48
  269.5 300.3 %reduce-scatter.4.cloned.1.call-done = bf16[768,1536]{0,1:T(8,128)(2,1)} async-done(((bf16[6144,1536]{0,1:T(8,128)(2,1)}), bf16[768,1536]{0,1:T(8,128)(2,1)}) %reduce-scatter.4.cloned.1.call-update) | async-done | bytes 2359312 | tf_op jit(solution)/shard_map/reduce_scatter | solution.py:84
  569.7 2.0 convert_element_type.64
  571.8 0.0 copy-start.1
  571.8 2.5 slice_multiply_fusion
  574.3 3.0 copy.45
  577.3 3.0 copy.44
  580.4 0.0 copy-done.1
Async XLA Ops:
  7.2 158.0 %copy-start = (bf16[1,6144,128]{2,1,0:T(8,128)(2,1)S(1)}, bf16[1,6144,128]{2,1,0:T(8,128)(2,1)}, u32[]{:S(2)}) copy-start(bf16[1,6144,128]{2,1,0:T(8,128)(2,1)} %param.16) | copy-start | bytes 4718596
  7.2 139.9 %all-gather.2.cloned.1.call-start = ((), (), s32[]{:S(2)}) async-start(), calls=%async_computation.3 | async-start | bytes 10616832 | tf_op jit(solution)/shard_map/all_gather | solution.py:73
  7.9 188.2 %all-reduce.2.cloned.1.call-start = ((), (), s32[]{:S(2)}) async-start(), calls=%async_computation.5 | async-start | bytes 262144 | tf_op jit(solution)/shard_map/psum | solution.py:99
  11.7 9.2 %copy-start.2 = (bf16[512,768]{0,1:T(8,128)(2,1)}, bf16[512,768]{0,1:T(8,128)(2,1)S(1)}, u32[]{:S(2)}) copy-start(bf16[512,768]{0,1:T(8,128)(2,1)S(1)} %copy.33) | copy-start | bytes 2359300
  159.2 4.9 copy-start.7
  163.2 0.9 copy-start.5
  165.1 100.6 %reduce-scatter.8.cloned.1.call-start = ((), (), s32[]{:S(2)}) async-start(), calls=%async_computation.7 | async-start | bytes 245760 | tf_op jit(solution)/shard_map/reduce_scatter | solution.py:110
  171.3 30.1 %copy-start.8 = (bf16[6,512,128]{1,2,0:T(8,128)(2,1)S(1)}, bf16[6,512,128]{1,2,0:T(8,128)(2,1)}, u32[]{:S(2)}) copy-start(bf16[6,512,128]{1,2,0:T(8,128)(2,1)} %fusion.24) | copy-start | bytes 2359300
  171.3 95.9 %reduce-scatter.6.cloned.1.call-start = ((), (), s32[]{:S(2)}) async-start(), calls=%async_computation.6 | async-start | bytes 1966080 | tf_op jit(solution)/shard_map/reduce_scatter | solution.py:107
  201.1 368.6 %reduce-scatter.4.cloned.1.call-start = ((), (), s32[]{:S(2)}) async-start(), calls=%async_computation.4 | async-start | bytes 21233664 | tf_op jit(solution)/shard_map/reduce_scatter | solution.py:84
  201.4 8.1 %copy-start.6 = (bf16[6,128,512]{2,1,0:T(8,128)(2,1)S(1)}, bf16[6,128,512]{2,1,0:T(8,128)(2,1)}, u32[]{:S(2)}) copy-start(bf16[6,128,512]{2,1,0:T(8,128)(2,1)} %copy-done.5) | copy-start | bytes 2359300
  238.9 3.7 copy-start.4
  242.6 11.0 %copy-start.3 = (bf16[512,768]{0,1:T(8,128)(2,1)S(1)}, bf16[512,768]{0,1:T(8,128)(2,1)}, u32[]{:S(2)}) copy-start(bf16[512,768]{0,1:T(8,128)(2,1)} %copy-done.2) | copy-start | bytes 2359300
  571.8 8.6 %copy-start.1 = (bf16[1,6144,128]{2,1,0:T(8,128)(2,1)S(1)}, bf16[1,6144,128]{2,1,0:T(8,128)(2,1)}, u32[]{:S(2)}) copy-start(bf16[1,6144,128]{2,1,0:T(8,128)(2,1)} %param.16) | copy-start | bytes 4718596
Sparse Core Ops, SparseCore 0:
  10.1 136.9 all-gather.1
  165.3 30.7 all-reduce.1
  198.4 15.7 reduce-scatter.7
  216.9 36.2 reduce-scatter.5
  256.9 312.7 reduce-scatter.3
where the time goes:
time: 590 us; the launch traced here: 587 us
  waiting for transfers between devices  447 us (76%)
  matrix products  78.6 us (13%)
  other arithmetic  29.3 us (5%)
  local copies, waits for them, and re-layouts  17.3 us (3%)
  between operations  13.9 us (2%)
    reduce_scatter x1, waiting for transfers between devices, local(): lax.psum_scatter(jnp.concatenate([out_term, value_term], axis=1).astype(j...  300 us
    all_gather x1, waiting for transfers between devices, local(): lax.all_gather(output_weight, ('section', 'dp'), axis=0, tiled=True)  122 us
    psum x1, waiting for transfers between devices, local(): mix_term = lax.psum(mix_part.astype(jnp.bfloat16), 'tensor')  24.7 us
    concatenate x1, other arithmetic, local(): jnp.concatenate([out_term, value_term], axis=1).astype(jnp.bfloat16)  21.3 us
    unnamed x26, local copies, waits for them, and re-layouts  15.9 us
  transfers between devices with their start and end apart: 5, of which 3 were waited for; matrix products, arithmetic and copies ran while one was open for 16% of the time, Pallas kernels for 0%

commit v1 on v0

v1 whole, which is shorter than its diff:
```python
import functools

import jax
import jax.numpy as jnp
from jax import lax
from jax.experimental import pallas as pl
from jax.experimental.pallas import tpu as pltpu
from jax.sharding import PartitionSpec as P

HD = 128
F32 = jnp.float32
BF16 = jnp.bfloat16
NT = (((1,), (1,)), ((), ()))
TN = (((0,), (0,)), ((), ()))


def dot(a, b, dims=(((1,), (0,)), ((), ()))):
    return lax.dot_general(a, b, dims, preferred_element_type=F32)


def probs_of(q, k, doc_col, doc_row):
    rows = q.shape[0]
    scores = dot(q, k, NT) * (HD ** -0.5)
    below = lax.broadcasted_iota(jnp.int32, (rows, rows), 0) >= lax.broadcasted_iota(
        jnp.int32, (rows, rows), 1
    )
    scores = jnp.where((doc_col == doc_row) & below, scores, F32(-1e30))
    expo = jnp.exp(scores - jnp.max(scores, axis=-1, keepdims=True))
    return expo / jnp.sum(expo, axis=-1, keepdims=True)


def output_kernel(q, k, v, doc_col, doc_row, out, half):
    probs = probs_of(q[...], k[...], doc_col[...], doc_row[...]).astype(BF16)
    half[0] = probs
    out[...] = dot(probs, v[...]).astype(BF16)


def value_kernel(half, g, out):
    out[...] = dot(half[0], g[...], TN).astype(BF16)


def score_kernel(q, k, v, g, doc_col, doc_row, grad_q, grad_k):
    probs = probs_of(q[...], k[...], doc_col[...], doc_row[...])
    grad_prob = dot(g[...], v[...], NT)
    row_delta = jnp.sum(probs * grad_prob, axis=-1, keepdims=True)
    grad_score = (probs * (grad_prob - row_delta) * (HD ** -0.5)).astype(BF16)
    grad_q[...] = dot(grad_score, k[...]).astype(BF16)
    grad_k[...] = dot(grad_score, q[...], TN).astype(BF16)


def attention_calls(rows, width):
    heads = width // HD
    head = pl.BlockSpec((rows, HD), lambda h: (0, h))
    col = pl.BlockSpec((rows, 1), lambda h: (0, 0))
    row = pl.BlockSpec((1, rows), lambda h: (0, 0))
    square = pl.BlockSpec((1, rows, rows), lambda h: (h, 0, 0))
    flat = jax.ShapeDtypeStruct((rows, width), BF16)
    params = pltpu.CompilerParams(vmem_limit_bytes=24 << 20)

    def call(kernel, in_specs, out_specs, out_shape, name, dots):
        return pl.pallas_call(
            kernel,
            grid=(heads,),
            in_specs=in_specs,
            out_specs=out_specs,
            out_shape=out_shape,
            compiler_params=params,
            name=name,
            cost_estimate=pl.CostEstimate(
                flops=dots * 2 * rows * rows * width,
                bytes_accessed=(len(in_specs) + 1) * rows * width * 2,
                transcendentals=heads * rows * rows,
            ),
        )

    forward = call(
        output_kernel,
        [head, head, head, col, row],
        (head, square),
        (flat, jax.ShapeDtypeStruct((heads, rows, rows), BF16)),
        "attend_out",
        2,
    )
    value = call(value_kernel, [square, head], head, flat, "value_grad", 1)
    scores = call(
        score_kernel,
        [head, head, head, head, col, row],
        (head, head),
        (flat, flat),
        "score_grads",
        4,
    )
    return forward, value, scores


def local(
    block_input,
    output_gradient,
    queries,
    saved_keys,
    values,
    document_index,
    output_weight,
    adapter_down_weight,
    adapter_up_weight,
):
    n_sec, n_dp, n_ten = (lax.axis_size(a) for a in ("section", "dp", "tensor"))
    sec, dp, ten = (lax.axis_index(a) for a in ("section", "dp", "tensor"))
    rows, width = block_input.shape
    local_width = queries.shape[1]
    part = width // n_sec
    piece = part // n_ten
    shard_rows = output_weight.shape[0]

    def shift(x, axis, by):
        size = lax.axis_size(axis)
        return lax.ppermute(x, axis, [(i, (i + by) % size) for i in range(size)])

    def columns(x, start, size):
        return lax.dynamic_slice_in_dim(x, start, size, 1)

    shards = []
    for k in range(n_dp):
        here = output_weight if k == 0 else shift(output_weight, "dp", k)
        shards.append((0, k, here))
        for j in range(1, n_sec):
            shards.append((j, k, shift(here, "section", j)))

    def regroup(x):
        gathered = [columns(x, sec * part, part)]
        for j in range(1, n_sec):
            sent = columns(x, ((sec + j) % n_sec) * part + ten * piece, piece)
            mine = shift(sent, "section", j)
            whole = jnp.zeros((rows, part), x.dtype)
            for m in range(n_ten):
                got = mine if m == 0 else shift(mine, "tensor", m)
                place = ((ten + n_ten - m) % n_ten) * piece
                whole = lax.dynamic_update_slice_in_dim(whole, got, place, 1)
            gathered.append(whole)
        return jnp.concatenate(gathered, axis=0)

    def across_sections(x):
        return jnp.concatenate([x] + [shift(x, "section", j) for j in range(1, n_sec)], axis=0)

    forward, value, scores = attention_calls(rows, local_width)
    doc_col, doc_row = document_index[:, None], document_index[None, :]
    output, probs_half = forward(queries, saved_keys, values, doc_col, doc_row)
    grad_rows = regroup(output_gradient)
    out_term = dot(grad_rows, across_sections(output), TN).astype(BF16)
    out_sum = lax.psum_scatter(out_term, "dp", scatter_dimension=0, tiled=True)

    attn_grad = jnp.zeros((rows, local_width), F32)
    for j, k, shard in shards:
        owner = ((sec + n_sec - j) % n_sec) * n_dp + (dp + n_dp - k) % n_dp
        attn_grad += dot(columns(output_gradient, owner * shard_rows, shard_rows), shard)
    attn_grad = attn_grad.astype(BF16)

    value_gradient = value(probs_half, attn_grad)
    value_term = dot(regroup(block_input), across_sections(value_gradient), TN).astype(BF16)
    value_sum = lax.psum_scatter(value_term, "dp", scatter_dimension=0, tiled=True)
    grad_query, grad_key = scores(
        queries, saved_keys, values, attn_grad, doc_col, doc_row
    )

    def sum_over_dp(blocks):
        take = functools.partial(lax.dynamic_index_in_dim, blocks, axis=0, keepdims=False)
        total = take(dp)
        for k in range(1, n_dp):
            total += shift(take((dp + k) % n_dp).astype(BF16), "dp", k).astype(F32)
        return total

    narrow = dot(block_input, adapter_down_weight[0]).astype(BF16)
    up_part = dot(narrow, value_gradient, TN)
    rank = up_part.shape[0]
    up_total = sum_over_dp(up_part.reshape(n_dp, rank // n_dp, local_width))

    mix = dot(value_gradient, adapter_up_weight[0], NT)
    mix_sent = mix.astype(BF16)
    for m in range(1, n_ten):
        mix += shift(mix_sent, "tensor", m).astype(F32)
    mix = mix.astype(BF16)
    out_rows = width // n_dp
    share = out_rows // n_ten
    strips = lax.dynamic_index_in_dim(
        block_input.reshape(rows, n_dp, n_ten, share), ten, 2, keepdims=False
    )
    down_part = dot(strips.reshape(rows, n_dp * share), mix, TN)
    down_mine = sum_over_dp(down_part.reshape(n_dp, share, rank))
    down_total = jnp.zeros((out_rows, rank), F32)
    for m in range(n_ten):
        got = down_mine if m == 0 else shift(down_mine, "tensor", m)
        place = ((ten + n_ten - m) % n_ten) * share
        down_total = lax.dynamic_update_slice_in_dim(down_total, got, place, 0)

    token_factor = (rows * n_sec * n_dp) ** (-0.5)
    adapter_factor = (rows * n_dp) ** (-0.5)
    return (
        out_sum.astype(F32) * token_factor,
        value_sum.astype(F32) * token_factor,
        grad_query,
        grad_key,
        (down_total * adapter_factor)[None],
        (up_total * adapter_factor)[None],
    )


def solution(mesh):
    return jax.shard_map(
        local,
        mesh=mesh,
        in_specs=(
            P(("section", "dp"), None),
            P(("section", "dp"), None),
            P(("section", "dp"), "tensor"),
            P(("section", "dp"), "tensor"),
            P(("section", "dp"), "tensor"),
            P(("section", "dp")),
            P(("section", "dp"), "tensor"),
            P("section", None, None),
            P("section", None, "tensor"),
        ),
        out_specs=(
            P(("section", "dp"), "tensor"),
            P(("section", "dp"), "tensor"),
            P(("section", "dp"), "tensor"),
            P(("section", "dp"), "tensor"),
            P("section", "dp", None),
            P("section", "dp", "tensor"),
        ),
        check_vma=False,
    )
```

time: 590 us -> 446 us (0.76)
  waiting for transfers between devices: 447 us -> 284 us
  matrix products: 78.6 us -> 44 us
  local copies, waits for them, and re-layouts: 17.3 us -> 47 us
  starting transfers between devices: 0.38 us -> 29.1 us
  other arithmetic: 29.3 us -> 8.21 us
  Pallas kernels: 0 us -> 17.2 us
    reduce_scatter x3 -> x2, waiting for transfers between devices: 300 us -> 12.6 us  [the longest x1 12.6 us: local(): lax.psum_scatter(value_term, 'dp', scatter_dimension=0, tiled=True)]
    ppermute x0 -> x29, waiting for transfers between devices: none -> 272 us  [shift(): return lax.ppermute(x, axis, [(i, (i + by) % size) for i in range(size)])]
    all_gather x1 -> x0, waiting for transfers between devices: 122 us -> none  [local(): lax.all_gather(output_weight, ('section', 'dp'), axis=0, tiled=True)]
    ppermute x0 -> x29, starting transfers between devices: none -> 29.1 us  [shift(): return lax.ppermute(x, axis, [(i, (i + by) % size) for i in range(size)])]
    dot_general x11 -> x13, matrix products: 72.1 us -> 44 us  [dot(): return lax.dot_general(a, b, dims, preferred_element_type=F32)]
    psum x1 -> x0, waiting for transfers between devices: 24.7 us -> none  [local(): mix_term = lax.psum(mix_part.astype(jnp.bfloat16), 'tensor')]
    concatenate x1 -> x0, other arithmetic: 21.3 us -> none  [local(): jnp.concatenate([out_term, value_term], axis=1).astype(jnp.bfloat16)]
    dynamic_slice x0 -> x6, local copies, waits for them, and re-layouts: none -> 20.7 us  [the longest x2 15.8 us: local(): lax.dynamic_index_in_dim(block_input.reshape(rows, n_dp, n_ten, share), t...]
  transfers between devices with their start and end apart: 5 -> 31, of which waited for: 3 -> 14; matrix products, arithmetic and copies ran while one was open for 16% -> 18% of each run, Pallas kernels for 0% -> 4%
where the time goes in v1:
time: 446 us; the launch traced here: 444 us
  waiting for transfers between devices  284 us (64%)
  local copies, waits for them, and re-layouts  47 us (11%)
  matrix products  44 us (10%)
  starting transfers between devices  29.1 us (7%)
  Pallas kernels  17.2 us (4%)
  between operations  14.5 us (3%)
  other arithmetic  8.21 us (2%)
    ppermute x29, waiting for transfers between devices, shift(): return lax.ppermute(x, axis, [(i, (i + by) % size) for i in range(size)])  272 us
    dot_general x13, matrix products, dot(): return lax.dot_general(a, b, dims, preferred_element_type=F32)  44 us
    ppermute x29, starting transfers between devices, shift(): return lax.ppermute(x, axis, [(i, (i + by) % size) for i in range(size)])  29.1 us
    dynamic_slice x2, local copies, waits for them, and re-layouts, local(): lax.dynamic_index_in_dim(block_input.reshape(rows, n_dp, n_ten, share), t...  15.8 us
    reshape x1, local copies, waits for them, and re-layouts, local(): block_input.reshape(rows, n_dp, n_ten, share)  13.5 us
    reduce_scatter x1, waiting for transfers between devices, local(): lax.psum_scatter(value_term, 'dp', scatter_dimension=0, tiled=True)  12.6 us
  transfers between devices with their start and end apart: 31, of which 14 were waited for; matrix products, arithmetic and copies ran while one was open for 18% of the time, Pallas kernels for 4%

profile of v1, /device:TPU:9, one launch (start us, length us, event | category | flops | bytes accessed | tf_op | source)
XLA Modules:
  0.0 444.3 jit_solution(1094449646994892866)
XLA Ops:
  7.2 1.3 constant_dynamic-slice_fusion.3
  8.5 1.3 collective-permute-start
  9.9 17.2 %collective-permute-done = bf16[512,768]{1,0:T(8,128)(2,1)S(1)} collective-permute-done((bf16[512,768]{1,0:T(8,128)(2,1)S(1)}, bf16[512,768]{1,0:T(8,128)(2,1)S(1)}, u32[]{:S(2)}, u32[]{:S(2)}) %collective-permute-start) | collective-permute-done | bytes 786464 | tf_op jit(solution)/shard_map/ppermute | solution.py:117
  27.0 2.6 collective-permute-start.1
  29.9 0.8 copy.16.doc_col
  31.4 1.1 copy-done.5
  32.6 1.1 copy-done.7
  33.7 1.1 copy-done.9
  34.8 6.7 %attend_out.1 = (bf16[512,768]{1,0:T(8,128)(2,1)S(1)}, bf16[6,512,512]{2,1,0:T(8,128)(2,1)S(1)}) custom-call(bf16[512,768]{1,0:T(8,128)(2,1)S(1)} %copy-done.5, bf16[512,768]{1,0:T(8,128)(2,1)S(1)} %copy-done.7, bf16[512,768]{1,0:T(8,128)(2,1)S(1)} %copy-done.9, s32[512,1]{1,0:T(8,128)S(1)} %copy.16.doc_col, s32[1,512]{1,0:T(1,128)S(1)} %bitcast.70), custom_call_target="tpu_custom_call" | custom-call | flops 805306368 | bytes 4718592 | tf_op jit(solution)/shard_map/attend_out/pallas_call | solution.py:147
  41.5 1.6 copy-done.1
  43.2 1.2 collective-permute-start.4
  44.9 2.1 constant_dynamic-slice_fusion.4
  47.5 1.2 constant_dynamic-update-slice_fusion.10
  48.7 15.4 %collective-permute-done.2 = bf16[512,768]{1,0:T(8,128)(2,1)} collective-permute-done((bf16[512,768]{1,0:T(8,128)(2,1)S(1)}, bf16[512,768]{1,0:T(8,128)(2,1)}, u32[]{:S(2)}, u32[]{:S(2)}) %collective-permute-start.2) | collective-permute-done | bytes 786464 | tf_op jit(solution)/shard_map/ppermute | solution.py:117
  64.1 1.2 constant_dynamic-update-slice_fusion.9
  65.5 8.1 %fusion.11 = bf16[3072,768]{1,0:T(8,128)(2,1)} fusion(bf16[512,3072]{1,0:T(8,128)(2,1)S(1)} %constant_dynamic-update-slice_fusion.8, bf16[512,3072]{1,0:T(8,128)(2,1)S(1)} %constant_dynamic-slice_fusion.4, bf16[512,768]{1,0:T(8,128)(2,1)} %collective-permute-done.4, bf16[512,768]{1,0:T(8,128)(2,1)S(1)} %get-tuple-element.10), kind=kOutput, calls=%fused_computation.9 | convolution fusion | flops 4849926144 | bytes 12582912 | tf_op jit(solution)/shard_map/dot_general | solution.py:18
  73.6 2.4 collective-permute-start.12
  76.0 1.5 collective-permute-start.14
  77.5 1.2 constant_dynamic-slice_fusion.1
  78.7 1.3 collective-permute-start.5
  80.2 86.0 %collective-permute-done.12 = bf16[768,768]{1,0:T(8,128)(2,1)} collective-permute-done((bf16[768,768]{1,0:T(8,128)(2,1)}, bf16[768,768]{1,0:T(8,128)(2,1)}, u32[]{:S(2)}, u32[]{:S(2)}) %collective-permute-start.12) | collective-permute-done | bytes 1179680 | tf_op jit(solution)/shard_map/ppermute | solution.py:117
  166.2 1.0 collective-permute-start.13
  167.2 3.5 fusion.43
  170.7 82.4 %collective-permute-done.10 = bf16[768,768]{1,0:T(8,128)(2,1)} collective-permute-done((bf16[768,768]{1,0:T(8,128)(2,1)}, bf16[768,768]{1,0:T(8,128)(2,1)}, u32[]{:S(2)}, u32[]{:S(2)}) %collective-permute-start.10) | collective-permute-done | bytes 1179680 | tf_op jit(solution)/shard_map/ppermute | solution.py:117
  253.1 1.2 collective-permute-start.11
  254.6 2.3 fusion.31
  256.9 2.3 fusion.35
  259.2 2.3 fusion.39
  261.8 2.3 fusion.41
  264.1 1.3 collective-permute-start.8
  265.4 2.3 fusion.33
  267.7 12.9 %collective-permute-done.11 = bf16[768,768]{1,0:T(8,128)(2,1)S(1)} collective-permute-done((bf16[768,768]{1,0:T(8,128)(2,1)}, bf16[768,768]{1,0:T(8,128)(2,1)S(1)}, u32[]{:S(2)}, u32[]{:S(2)}) %collective-permute-start.11) | collective-permute-done | bytes 1179680 | tf_op jit(solution)/shard_map/ppermute | solution.py:117
  280.6 2.1 fusion.37
  282.7 23.2 %collective-permute-done.15 = bf16[768,768]{1,0:T(8,128)(2,1)S(1)} collective-permute-done((bf16[768,768]{1,0:T(8,128)(2,1)}, bf16[768,768]{1,0:T(8,128)(2,1)S(1)}, u32[]{:S(2)}, u32[]{:S(2)}) %collective-permute-start.15) | collective-permute-done | bytes 1179680 | tf_op jit(solution)/shard_map/ppermute | solution.py:117
  305.9 2.1 add_convert_fusion.g
  308.0 2.4 value_grad.1
  310.4 1.3 collective-permute-start.16
  312.3 1.2 constant_dynamic-update-slice_fusion.7
  313.9 14.4 %collective-permute-done.16 = bf16[512,768]{1,0:T(8,128)(2,1)S(1)} collective-permute-done((bf16[512,768]{1,0:T(8,128)(2,1)S(1)}, bf16[512,768]{1,0:T(8,128)(2,1)S(1)}, u32[]{:S(2)}, u32[]{:S(2)}) %collective-permute-start.16) | collective-permute-done | bytes 786464 | tf_op jit(solution)/shard_map/ppermute | solution.py:117
  328.4 7.0 %fusion.8 = bf16[3072,768]{1,0:T(8,128)(2,1)} fusion(bf16[512,3072]{1,0:T(8,128)(2,1)S(1)} %constant_dynamic-update-slice_fusion.4, bf16[512,3072]{1,0:T(8,128)(2,1)S(1)} %constant_dynamic-slice_fusion.2, bf16[512,768]{1,0:T(8,128)(2,1)S(1)} %collective-permute-done.16, bf16[512,768]{1,0:T(8,128)(2,1)S(1)} %value_grad.1), kind=kOutput, calls=%fused_computation.8 | convolution fusion | flops 4849926144 | bytes 12582912 | tf_op jit(solution)/shard_map/dot_general | solution.py:18
  335.4 13.5 %reshape.30 = bf16[512,4,4,384]{3,2,1,0:T(4,128)(2,1)} reshape(bf16[512,6144]{1,0:T(8,128)(2,1)} %param.9) | data formatting | bytes 12582912 | tf_op jit(solution)/shard_map/reshape | solution.py:185
  348.8 7.7 %constant_dynamic-slice_fusion = bf16[512,4,1,384]{3,2,1,0:T(2,128)(2,1)} fusion(bf16[512,4,4,384]{3,2,1,0:T(4,128)(2,1)} %reshape.30, s32[]{:T(128)S(6)} %select_n.201), kind=kLoop, calls=%fused_computation.69 | loop fusion | bytes 3145732 | tf_op jit(solution)/shard_map/jit(dynamic_index_in_dim)/dynamic_slice | solution.py:184
  356.5 8.2 %copy.18 = bf16[512,4,1,384]{0,3,1,2:T(8,128)(2,1)} copy(bf16[512,4,1,384]{3,2,1,0:T(2,128)(2,1)} %constant_dynamic-slice_fusion) | data formatting | bytes 3145728 | tf_op jit(solution)/shard_map/jit(dynamic_index_in_dim)/dynamic_slice | solution.py:184
  364.7 2.0 fusion.72
  366.7 2.2 collective-permute-start.17
  368.9 1.3 collective-permute-start.18
  370.2 5.7 %fusion.28 = f32[128,768]{1,0:T(8,128)} fusion(bf16[512,768]{1,0:T(8,128)(2,1)S(1)} %value_grad.1, bf16[512,6144]{1,0:T(8,128)(2,1)} %param.9, bf16[1,6144,128]{2,1,0:T(8,128)(2,1)S(1)} %copy-done), kind=kOutput, calls=%fused_computation.24 | convolution fusion | flops 906035200 | bytes 9043968 | tf_op jit(solution)/shard_map/dot_general | solution.py:18
  375.9 1.2 fusion.58
  377.1 2.0 collective-permute-start.26
  379.2 2.1 fusion.20
  382.0 2.7 collective-permute-start.21
  385.2 8.1 %score_grads.1 = (bf16[512,768]{1,0:T(8,128)(2,1)}, bf16[512,768]{1,0:T(8,128)(2,1)}) custom-call(bf16[512,768]{1,0:T(8,128)(2,1)S(1)} %copy-done.6, bf16[512,768]{1,0:T(8,128)(2,1)S(1)} %copy-done.8, bf16[512,768]{1,0:T(8,128)(2,1)S(1)} %copy-done.10, bf16[512,768]{1,0:T(8,128)(2,1)S(1)} %add_convert_fusion.g, s32[512,1]{1,0:T(8,128)S(1)} %copy.16.doc_col, ...), custom_call_target="tpu_custom_call" | custom-call | flops 1610612736 | bytes 5505024 | tf_op jit(solution)/shard_map/score_grads/pallas_call | solution.py:161
  393.3 5.2 %collective-permute-done.20 = bf16[384,128]{1,0:T(8,128)(2,1)S(1)} collective-permute-done((bf16[384,128]{1,0:T(8,128)(2,1)S(1)}, bf16[384,128]{1,0:T(8,128)(2,1)S(1)}, u32[]{:S(2)}, u32[]{:S(2)}) %collective-permute-start.20) | collective-permute-done | bytes 98336 | tf_op jit(solution)/shard_map/ppermute | solution.py:117
  398.5 7.9 %collective-permute-done.21 = bf16[384,128]{1,0:T(8,128)(2,1)S(1)} collective-permute-done((bf16[384,128]{1,0:T(8,128)(2,1)S(1)}, bf16[384,128]{1,0:T(8,128)(2,1)S(1)}, u32[]{:S(2)}, u32[]{:S(2)}) %collective-permute-start.21) | collective-permute-done | bytes 98336 | tf_op jit(solution)/shard_map/ppermute | solution.py:117
  406.5 2.1 collective-permute-start.23
  408.7 1.1 collective-permute-done.28
  409.7 1.6 fusion.57
  411.3 0.9 collective-permute-start.25
  412.8 4.7 %collective-permute-done.24 = f32[384,128]{1,0:T(8,128)S(1)} collective-permute-done((f32[384,128]{1,0:T(8,128)S(1)}, f32[384,128]{1,0:T(8,128)S(1)}, u32[]{:S(2)}, u32[]{:S(2)}) %collective-permute-start.24) | collective-permute-done | bytes 196640 | tf_op jit(solution)/shard_map/ppermute | solution.py:117
  417.4 0.9 collective-permute-done.25
  418.3 0.9 multiply_bitcast_fusion
  419.3 2.8 convert_multiply_fusion.1
  422.1 12.6 %reduce-scatter.5.cloned.1.call-done = bf16[768,768]{1,0:T(8,128)(2,1)} async-done(((bf16[3072,768]{1,0:T(8,128)(2,1)}), bf16[768,768]{1,0:T(8,128)(2,1)}) %reduce-scatter.5.cloned.1.call-update) | async-done | bytes 1179664 | tf_op jit(solution)/shard_map/reduce_scatter | solution.py:160
  434.7 2.8 convert_multiply_fusion
  (74 shorter events, 5.8 us)
Async XLA Ops:
  7.2 363.0 %copy-start = (bf16[1,6144,128]{2,1,0:T(8,128)(2,1)S(1)}, bf16[1,6144,128]{2,1,0:T(8,128)(2,1)}, u32[]{:S(2)}) copy-start(bf16[1,6144,128]{2,1,0:T(8,128)(2,1)} %param.16) | copy-start | bytes 4718596
  7.2 412.1 %reduce-scatter.3.cloned.1.call-start = ((), (), s32[]{:S(2)}) async-start(), calls=%async_computation.2 | async-start | bytes 5898240 | tf_op jit(solution)/shard_map/reduce_scatter | solution.py:150
  8.5 18.5 %collective-permute-start = (bf16[512,768]{1,0:T(8,128)(2,1)S(1)}, bf16[512,768]{1,0:T(8,128)(2,1)S(1)}, u32[]{:S(2)}, u32[]{:S(2)}) collective-permute-start(bf16[512,768]{1,0:T(8,128)(2,1)S(1)} %constant_dynamic-slice_fusion.3), channel_id=1, source_target_pairs={{0,4},{4,0},{1,5},{5,1},{2,6},{6,2},{3,7},{7,3},{8,12},{12,8},{9,1... | collective-permute-start | bytes 2359304 | tf_op jit(solution)/shard_map/ppermute | solution.py:117
  27.0 20.4 %collective-permute-start.1 = (bf16[512,768]{1,0:T(8,128)(2,1)S(1)}, bf16[512,768]{1,0:T(8,128)(2,1)}, u32[]{:S(2)}, u32[]{:S(2)}) collective-permute-start(bf16[512,768]{1,0:T(8,128)(2,1)S(1)} %collective-permute-done), channel_id=1, source_target_pairs={{0,8},{8,16},{16,24},{24,0},{1,9},{9,17},{17,25},{25,1},{2,10},{10... | collective-permute-start | bytes 2359304 | tf_op jit(solution)/shard_map/ppermute | solution.py:117
  29.7 34.5 %collective-permute-start.2 = (bf16[512,768]{1,0:T(8,128)(2,1)S(1)}, bf16[512,768]{1,0:T(8,128)(2,1)}, u32[]{:S(2)}, u32[]{:S(2)}) collective-permute-start(bf16[512,768]{1,0:T(8,128)(2,1)S(1)} %collective-permute-done), channel_id=1, source_target_pairs={{0,16},{8,24},{16,0},{24,8},{1,17},{9,25},{17,1},{25,9},{2,18},{10... | collective-permute-start | bytes 2359304 | tf_op jit(solution)/shard_map/ppermute | solution.py:117
  30.7 0.7 copy-start.3
  31.4 1.1 copy-start.5
  32.6 1.1 copy-start.7
  33.7 1.1 copy-start.9
  41.5 1.6 copy-start.1
  43.2 22.3 %collective-permute-start.4 = (bf16[512,768]{1,0:T(8,128)(2,1)S(1)}, bf16[512,768]{1,0:T(8,128)(2,1)}, u32[]{:S(2)}, u32[]{:S(2)}) collective-permute-start(bf16[512,768]{1,0:T(8,128)(2,1)S(1)} %get-tuple-element.10), channel_id=1, source_target_pairs={{0,4},{4,0},{1,5},{5,1},{2,6},{6,2},{3,7},{7,3},{8,12},{12,8},{9,1... | collective-permute-start | bytes 2359304 | tf_op jit(solution)/shard_map/ppermute | solution.py:117
  44.4 21.0 %collective-permute-start.3 = (bf16[512,768]{1,0:T(8,128)(2,1)S(1)}, bf16[512,768]{1,0:T(8,128)(2,1)S(1)}, u32[]{:S(2)}, u32[]{:S(2)}) collective-permute-start(bf16[512,768]{1,0:T(8,128)(2,1)S(1)} %collective-permute-done), channel_id=1, source_target_pairs={{0,24},{8,0},{16,8},{24,16},{1,25},{9,1},{17,9},{25,17},{2,26},{10... | collective-permute-start | bytes 2359304 | tf_op jit(solution)/shard_map/ppermute | solution.py:117
  73.6 361.1 %reduce-scatter.5.cloned.1.call-start = ((), (), s32[]{:S(2)}) async-start(), calls=%async_computation.3 | async-start | bytes 5898240 | tf_op jit(solution)/shard_map/reduce_scatter | solution.py:160
  73.6 92.5 %collective-permute-start.12 = (bf16[768,768]{1,0:T(8,128)(2,1)}, bf16[768,768]{1,0:T(8,128)(2,1)}, u32[]{:S(2)}, u32[]{:S(2)}) collective-permute-start(bf16[768,768]{1,0:T(8,128)(2,1)} %param.15), channel_id=1, source_target_pairs={{0,2},{1,3},{2,0},{3,1},{4,6},{5,7},{6,4},{7,5},{8,10},{9,11},{10,... | collective-permute-start | bytes 3538952 | tf_op jit(solution)/shard_map/ppermute | solution.py:117
  76.0 177.1 %collective-permute-start.10 = (bf16[768,768]{1,0:T(8,128)(2,1)}, bf16[768,768]{1,0:T(8,128)(2,1)}, u32[]{:S(2)}, u32[]{:S(2)}) collective-permute-start(bf16[768,768]{1,0:T(8,128)(2,1)} %param.15), channel_id=1, source_target_pairs={{0,1},{1,2},{2,3},{3,0},{4,5},{5,6},{6,7},{7,4},{8,9},{9,10},{10,1... | collective-permute-start | bytes 3538952 | tf_op jit(solution)/shard_map/ppermute | solution.py:117
  76.0 178.3 %collective-permute-start.14 = (bf16[768,768]{1,0:T(8,128)(2,1)}, bf16[768,768]{1,0:T(8,128)(2,1)}, u32[]{:S(2)}, u32[]{:S(2)}) collective-permute-start(bf16[768,768]{1,0:T(8,128)(2,1)} %param.15), channel_id=1, source_target_pairs={{0,3},{1,0},{2,1},{3,2},{4,7},{5,4},{6,5},{7,6},{8,11},{9,8},{10,9... | collective-permute-start | bytes 3538952 | tf_op jit(solution)/shard_map/ppermute | solution.py:117
  78.7 92.0 %collective-permute-start.5 = (bf16[512,768]{1,0:T(8,128)(2,1)S(1)}, bf16[512,768]{1,0:T(8,128)(2,1)}, u32[]{:S(2)}, u32[]{:S(2)}) collective-permute-start(bf16[512,768]{1,0:T(8,128)(2,1)S(1)} %constant_dynamic-slice_fusion.1), channel_id=1, source_target_pairs={{0,4},{4,0},{1,5},{5,1},{2,6},{6,2},{3,7},{7,3},{8,12},{12,8},{9,1... | collective-permute-start | bytes 2359304 | tf_op jit(solution)/shard_map/ppermute | solution.py:117
  80.0 181.5 %collective-permute-start.9 = (bf16[768,768]{1,0:T(8,128)(2,1)}, bf16[768,768]{1,0:T(8,128)(2,1)}, u32[]{:S(2)}, u32[]{:S(2)}) collective-permute-start(bf16[768,768]{1,0:T(8,128)(2,1)} %param.15), channel_id=1, source_target_pairs={{0,4},{4,0},{1,5},{5,1},{2,6},{6,2},{3,7},{7,3},{8,12},{12,8},{9,1... | collective-permute-start | bytes 3538952 | tf_op jit(solution)/shard_map/ppermute | solution.py:117
  166.2 97.9 %collective-permute-start.13 = (bf16[768,768]{1,0:T(8,128)(2,1)}, bf16[768,768]{1,0:T(8,128)(2,1)}, u32[]{:S(2)}, u32[]{:S(2)}) collective-permute-start(bf16[768,768]{1,0:T(8,128)(2,1)} %collective-permute-done.12), channel_id=1, source_target_pairs={{0,4},{4,0},{1,5},{5,1},{2,6},{6,2},{3,7},{7,3},{8,12},{12,8},{9,1... | collective-permute-start | bytes 3538952 | tf_op jit(solution)/shard_map/ppermute | solution.py:117
  170.7 142.9 %collective-permute-start.6 = (bf16[512,768]{1,0:T(8,128)(2,1)}, bf16[512,768]{1,0:T(8,128)(2,1)S(1)}, u32[]{:S(2)}, u32[]{:S(2)}) collective-permute-start(bf16[512,768]{1,0:T(8,128)(2,1)} %collective-permute-done.5), channel_id=1, source_target_pairs={{0,8},{8,16},{16,24},{24,0},{1,9},{9,17},{17,25},{25,1},{2,10},{10... | collective-permute-start | bytes 2359304 | tf_op jit(solution)/shard_map/ppermute | solution.py:117
  253.1 27.5 %collective-permute-start.11 = (bf16[768,768]{1,0:T(8,128)(2,1)}, bf16[768,768]{1,0:T(8,128)(2,1)S(1)}, u32[]{:S(2)}, u32[]{:S(2)}) collective-permute-start(bf16[768,768]{1,0:T(8,128)(2,1)} %collective-permute-done.10), channel_id=1, source_target_pairs={{0,4},{4,0},{1,5},{5,1},{2,6},{6,2},{3,7},{7,3},{8,12},{12,8},{9,1... | collective-permute-start | bytes 3538952 | tf_op jit(solution)/shard_map/ppermute | solution.py:117
  254.3 51.5 %collective-permute-start.15 = (bf16[768,768]{1,0:T(8,128)(2,1)}, bf16[768,768]{1,0:T(8,128)(2,1)S(1)}, u32[]{:S(2)}, u32[]{:S(2)}) collective-permute-start(bf16[768,768]{1,0:T(8,128)(2,1)} %collective-permute-done.14), channel_id=1, source_target_pairs={{0,4},{4,0},{1,5},{5,1},{2,6},{6,2},{3,7},{7,3},{8,12},{12,8},{9,1... | collective-permute-start | bytes 3538952 | tf_op jit(solution)/shard_map/ppermute | solution.py:117
  261.5 52.2 %collective-permute-start.7 = (bf16[512,768]{1,0:T(8,128)(2,1)}, bf16[512,768]{1,0:T(8,128)(2,1)S(1)}, u32[]{:S(2)}, u32[]{:S(2)}) collective-permute-start(bf16[512,768]{1,0:T(8,128)(2,1)} %collective-permute-done.5), channel_id=1, source_target_pairs={{0,16},{8,24},{16,0},{24,8},{1,17},{9,25},{17,1},{25,9},{2,18},{10... | collective-permute-start | bytes 2359304 | tf_op jit(solution)/shard_map/ppermute | solution.py:117
  264.1 41.8 %copy-start.11 = (f32[512,768]{1,0:T(8,128)S(1)}, f32[512,768]{1,0:T(8,128)}, u32[]{:S(2)}) copy-start(f32[512,768]{1,0:T(8,128)} %fusion.43) | copy-start | bytes 4718596
  264.1 49.7 %collective-permute-start.8 = (bf16[512,768]{1,0:T(8,128)(2,1)}, bf16[512,768]{1,0:T(8,128)(2,1)S(1)}, u32[]{:S(2)}, u32[]{:S(2)}) collective-permute-start(bf16[512,768]{1,0:T(8,128)(2,1)} %collective-permute-done.5), channel_id=1, source_target_pairs={{0,24},{8,0},{16,8},{24,16},{1,25},{9,1},{17,9},{25,17},{2,26},{10... | collective-permute-start | bytes 2359304 | tf_op jit(solution)/shard_map/ppermute | solution.py:117
  280.6 31.1 %slice-start = ((s8[6291456]{0:T(1024)(128)(4,1)}), s8[4194304]{0:T(1024)(128)(4,1)S(1)}, s32[]{:S(2)}) async-start(s8[6291456]{0:T(1024)(128)(4,1)} %bitcast.72), calls=%async_computation.4 | async-start | bytes 8388608
  282.7 25.3 %copy-start.2 = (bf16[6,512,512]{2,1,0:T(8,128)(2,1)S(1)}, bf16[6,512,512]{2,1,0:T(8,128)(2,1)}, u32[]{:S(2)}) copy-start(bf16[6,512,512]{2,1,0:T(8,128)(2,1)} %copy-done.1) | copy-start | bytes 9437188
  282.7 29.0 %slice-start.1 = ((s8[6291456]{0:T(1024)(128)(4,1)}), s8[2097152]{0:T(1024)(128)(4,1)S(1)}, s32[]{:S(2)}) async-start(s8[6291456]{0:T(1024)(128)(4,1)} %bitcast.72), calls=%async_computation.5 | async-start | bytes 4194304
  310.4 18.0 %collective-permute-start.16 = (bf16[512,768]{1,0:T(8,128)(2,1)S(1)}, bf16[512,768]{1,0:T(8,128)(2,1)S(1)}, u32[]{:S(2)}, u32[]{:S(2)}) collective-permute-start(bf16[512,768]{1,0:T(8,128)(2,1)S(1)} %value_grad.1), channel_id=1, source_target_pairs={{0,4},{4,0},{1,5},{5,1},{2,6},{6,2},{3,7},{7,3},{8,12},{12,8},{9,1... | collective-permute-start | bytes 2359304 | tf_op jit(solution)/shard_map/ppermute | solution.py:117
  366.7 12.4 %collective-permute-start.17 = (bf16[512,128]{1,0:T(8,128)(2,1)}, bf16[512,128]{1,0:T(8,128)(2,1)S(1)}, u32[]{:S(2)}, u32[]{:S(2)}) collective-permute-start(bf16[512,128]{1,0:T(8,128)(2,1)} %get-tuple-element.22), channel_id=1, source_target_pairs={{0,8},{8,16},{16,24},{24,0},{1,9},{9,17},{17,25},{25,1},{2,10},{10... | collective-permute-start | bytes 393224 | tf_op jit(solution)/shard_map/ppermute | solution.py:117
  368.9 10.3 %collective-permute-start.18 = (bf16[512,128]{1,0:T(8,128)(2,1)}, bf16[512,128]{1,0:T(8,128)(2,1)}, u32[]{:S(2)}, u32[]{:S(2)}) collective-permute-start(bf16[512,128]{1,0:T(8,128)(2,1)} %get-tuple-element.22), channel_id=1, source_target_pairs={{0,16},{8,24},{16,0},{24,8},{1,17},{9,25},{17,1},{25,9},{2,18},{10... | collective-permute-start | bytes 393224 | tf_op jit(solution)/shard_map/ppermute | solution.py:117
  370.2 9.0 %collective-permute-start.19 = (bf16[512,128]{1,0:T(8,128)(2,1)}, bf16[512,128]{1,0:T(8,128)(2,1)}, u32[]{:S(2)}, u32[]{:S(2)}) collective-permute-start(bf16[512,128]{1,0:T(8,128)(2,1)} %get-tuple-element.22), channel_id=1, source_target_pairs={{0,24},{8,0},{16,8},{24,16},{1,25},{9,1},{17,9},{25,17},{2,26},{10... | collective-permute-start | bytes 393224 | tf_op jit(solution)/shard_map/ppermute | solution.py:117
  375.9 9.3 %copy-start.4 = (s32[512]{0:T(512)S(1)}, s32[512]{0:T(512)}, u32[]{:S(2)}) copy-start(s32[512]{0:T(512)} %param.14) | copy-start | bytes 6148
  375.9 9.3 %copy-start.6 = (bf16[512,768]{1,0:T(8,128)(2,1)S(1)}, bf16[512,768]{1,0:T(8,128)(2,1)}, u32[]{:S(2)}) copy-start(bf16[512,768]{1,0:T(8,128)(2,1)} %q.3) | copy-start | bytes 2359300
  375.9 9.3 %copy-start.8 = (bf16[512,768]{1,0:T(8,128)(2,1)S(1)}, bf16[512,768]{1,0:T(8,128)(2,1)}, u32[]{:S(2)}) copy-start(bf16[512,768]{1,0:T(8,128)(2,1)} %k.3) | copy-start | bytes 2359300
  375.9 9.3 %copy-start.10 = (bf16[512,768]{1,0:T(8,128)(2,1)S(1)}, bf16[512,768]{1,0:T(8,128)(2,1)}, u32[]{:S(2)}) copy-start(bf16[512,768]{1,0:T(8,128)(2,1)} %v.3) | copy-start | bytes 2359300
  377.1 31.6 %collective-permute-start.26 = (bf16[32,768]{1,0:T(8,128)(2,1)S(1)}, bf16[32,768]{1,0:T(8,128)(2,1)S(1)}, u32[]{:S(2)}, u32[]{:S(2)}) collective-permute-start(bf16[32,768]{1,0:T(8,128)(2,1)S(1)} %get-tuple-element.19), channel_id=1, source_target_pairs={{0,1},{1,2},{2,3},{3,0},{4,5},{5,6},{6,7},{7,4},{8,9},{9,10},{10,1... | collective-permute-start | bytes 147464 | tf_op jit(solution)/shard_map/ppermute | solution.py:117
  379.1 29.5 %collective-permute-start.27 = (bf16[32,768]{1,0:T(8,128)(2,1)S(1)}, bf16[32,768]{1,0:T(8,128)(2,1)S(1)}, u32[]{:S(2)}, u32[]{:S(2)}) collective-permute-start(bf16[32,768]{1,0:T(8,128)(2,1)S(1)} %get-tuple-element.21), channel_id=1, source_target_pairs={{0,2},{1,3},{2,0},{3,1},{4,6},{5,7},{6,4},{7,5},{8,10},{9,11},{10,... | collective-permute-start | bytes 147464 | tf_op jit(solution)/shard_map/ppermute | solution.py:117
  381.3 17.1 %collective-permute-start.20 = (bf16[384,128]{1,0:T(8,128)(2,1)S(1)}, bf16[384,128]{1,0:T(8,128)(2,1)S(1)}, u32[]{:S(2)}, u32[]{:S(2)}) collective-permute-start(bf16[384,128]{1,0:T(8,128)(2,1)S(1)} %get-tuple-element.16), channel_id=1, source_target_pairs={{0,1},{1,2},{2,3},{3,0},{4,5},{5,6},{6,7},{7,4},{8,9},{9,10},{10,1... | collective-permute-start | bytes 294920 | tf_op jit(solution)/shard_map/ppermute | solution.py:117
  382.0 24.4 %collective-permute-start.21 = (bf16[384,128]{1,0:T(8,128)(2,1)S(1)}, bf16[384,128]{1,0:T(8,128)(2,1)S(1)}, u32[]{:S(2)}, u32[]{:S(2)}) collective-permute-start(bf16[384,128]{1,0:T(8,128)(2,1)S(1)} %get-tuple-element.18), channel_id=1, source_target_pairs={{0,2},{1,3},{2,0},{3,1},{4,6},{5,7},{6,4},{7,5},{8,10},{9,11},{10,... | collective-permute-start | bytes 294920 | tf_op jit(solution)/shard_map/ppermute | solution.py:117
  384.7 21.7 %collective-permute-start.22 = (bf16[384,128]{1,0:T(8,128)(2,1)S(1)}, bf16[384,128]{1,0:T(8,128)(2,1)S(1)}, u32[]{:S(2)}, u32[]{:S(2)}) collective-permute-start(bf16[384,128]{1,0:T(8,128)(2,1)S(1)} %get-tuple-element.17), channel_id=1, source_target_pairs={{0,3},{1,0},{2,1},{3,2},{4,7},{5,4},{6,5},{7,6},{8,11},{9,8},{10,9... | collective-permute-start | bytes 294920 | tf_op jit(solution)/shard_map/ppermute | solution.py:117
  398.5 11.2 %collective-permute-start.28 = (bf16[32,768]{1,0:T(8,128)(2,1)S(1)}, bf16[32,768]{1,0:T(8,128)(2,1)S(1)}, u32[]{:S(2)}, u32[]{:S(2)}) collective-permute-start(bf16[32,768]{1,0:T(8,128)(2,1)S(1)} %get-tuple-element.20), channel_id=1, source_target_pairs={{0,3},{1,0},{2,1},{3,2},{4,7},{5,4},{6,5},{7,6},{8,11},{9,8},{10,9... | collective-permute-start | bytes 147464 | tf_op jit(solution)/shard_map/ppermute | solution.py:117
  406.5 6.2 %collective-permute-start.23 = (f32[384,128]{1,0:T(8,128)S(1)}, f32[384,128]{1,0:T(8,128)S(1)}, u32[]{:S(2)}, u32[]{:S(2)}) collective-permute-start(f32[384,128]{1,0:T(8,128)S(1)} %get-tuple-element.15), channel_id=1, source_target_pairs={{0,8},{8,16},{16,24},{24,0},{1,9},{9,17},{17,25},{25,1},{2,10},{10... | collective-permute-start | bytes 589832 | tf_op jit(solution)/shard_map/ppermute | solution.py:117
  408.6 8.8 %collective-permute-start.24 = (f32[384,128]{1,0:T(8,128)S(1)}, f32[384,128]{1,0:T(8,128)S(1)}, u32[]{:S(2)}, u32[]{:S(2)}) collective-permute-start(f32[384,128]{1,0:T(8,128)S(1)} %get-tuple-element.15), channel_id=1, source_target_pairs={{0,16},{8,24},{16,0},{24,8},{1,17},{9,25},{17,1},{25,9},{2,18},{10... | collective-permute-start | bytes 589832 | tf_op jit(solution)/shard_map/ppermute | solution.py:117
  411.3 7.0 %collective-permute-start.25 = (f32[384,128]{1,0:T(8,128)S(1)}, f32[384,128]{1,0:T(8,128)S(1)}, u32[]{:S(2)}, u32[]{:S(2)}) collective-permute-start(f32[384,128]{1,0:T(8,128)S(1)} %get-tuple-element.15), channel_id=1, source_target_pairs={{0,24},{8,0},{16,8},{24,16},{1,25},{9,1},{17,9},{25,17},{2,26},{10... | collective-permute-start | bytes 589832 | tf_op jit(solution)/shard_map/ppermute | solution.py:117
Sparse Core Ops, SparseCore 0:
  73.7 174.8 reduce-scatter.2
  335.5 99.1 reduce-scatter.4

commit v2 on v1

--- a/solution.py
+++ b/solution.py
@@ -119,12 +119,42 @@
     def columns(x, start, size):
         return lax.dynamic_slice_in_dim(x, start, size, 1)
 
-    shards = []
-    for k in range(n_dp):
-        here = output_weight if k == 0 else shift(output_weight, "dp", k)
-        shards.append((0, k, here))
-        for j in range(1, n_sec):
-            shards.append((j, k, shift(here, "section", j)))
+    def step(x, by):
+        pairs = [(i, i + by) for i in range(n_dp) if 0 <= i + by < n_dp]
+        return lax.ppermute(x, "dp", pairs)
+
+    order = [
+        sorted((d - o for o in range(n_dp) if o != d), key=lambda hop: (abs(hop), hop < 0))
+        for d in range(n_dp)
+    ]
+
+    def pick(choices, values):
+        out = values[choices[0]]
+        for hop in sorted(set(choices) - {choices[0]}):
+            held = functools.reduce(
+                jnp.logical_or, [dp == d for d in range(n_dp) if choices[d] == hop]
+            )
+            out = jnp.where(held, values[hop], out)
+        return out
+
+    def forwards(x):
+        return [shift(x, "section", j) for j in range(1, n_sec)]
+
+    arrivals = {0: output_weight}
+    slots = [(dp, output_weight, forwards(output_weight))]
+    below, above = output_weight, output_weight
+    for k in range(1, n_dp):
+        below, above = step(below, 1), step(above, -1)
+        arrivals[k], arrivals[-k] = below, above
+        choices = [order[d][k - 1] for d in range(n_dp)]
+        sent = slots[k - 2][2] if k > 1 else []
+        here, below, above, sent = lax.optimization_barrier(
+            (pick(choices, arrivals), below, above, sent)
+        )
+        if k > 1:
+            slots[k - 2] = (*slots[k - 2][:2], sent)
+        hops = {hop: jnp.int32(hop) for hop in arrivals}
+        slots.append((dp - pick(choices, hops), here, forwards(here)))
 
     def regroup(x):
         gathered = [columns(x, sec * part, part)]
@@ -146,13 +176,17 @@
     doc_col, doc_row = document_index[:, None], document_index[None, :]
     output, probs_half = forward(queries, saved_keys, values, doc_col, doc_row)
     grad_rows = regroup(output_gradient)
-    out_term = dot(grad_rows, across_sections(output), TN).astype(BF16)
+    output_rows, kept = lax.optimization_barrier(
+        (across_sections(output), [here for _, here, _ in slots])
+    )
+    out_term = dot(grad_rows, output_rows, TN).astype(BF16)
     out_sum = lax.psum_scatter(out_term, "dp", scatter_dimension=0, tiled=True)
 
     attn_grad = jnp.zeros((rows, local_width), F32)
-    for j, k, shard in shards:
-        owner = ((sec + n_sec - j) % n_sec) * n_dp + (dp + n_dp - k) % n_dp
-        attn_grad += dot(columns(output_gradient, owner * shard_rows, shard_rows), shard)
+    for (owner_dp, _, sent), here in zip(slots, kept):
+        for j, shard in enumerate([here] + list(sent)):
+            owner = ((sec + n_sec - j) % n_sec) * n_dp + owner_dp
+            attn_grad += dot(columns(output_gradient, owner * shard_rows, shard_rows), shard)
     attn_grad = attn_grad.astype(BF16)
 
     value_gradient = value(probs_half, attn_grad)
@@ -181,10 +215,10 @@
     mix = mix.astype(BF16)
     out_rows = width // n_dp
     share = out_rows // n_ten
-    strips = lax.dynamic_index_in_dim(
-        block_input.reshape(rows, n_dp, n_ten, share), ten, 2, keepdims=False
-    )
-    down_part = dot(strips.reshape(rows, n_dp * share), mix, TN)
+    strips = jnp.concatenate(
+        [columns(block_input, k * out_rows + ten * share, share) for k in range(n_dp)], axis=1
+    )
+    down_part = dot(strips, mix, TN)
     down_mine = sum_over_dp(down_part.reshape(n_dp, share, rank))
     down_total = jnp.zeros((out_rows, rank), F32)
     for m in range(n_ten):

time: 446 us -> 364 us (0.82)
  waiting for transfers between devices: 284 us -> 198 us
  local copies, waits for them, and re-layouts: 47 us -> 20.5 us
  starting transfers between devices: 29.1 us -> 55.3 us
  other arithmetic: 8.21 us -> 15.9 us
    ppermute x29 -> x26, waiting for transfers between devices: 272 us -> 133 us  [shift(): return lax.ppermute(x, axis, [(i, (i + by) % size) for i in range(size)])]
    reduce_scatter x1, waiting for transfers between devices: 12.6 us -> 39.4 us  [local(): lax.psum_scatter(value_term, 'dp', scatter_dimension=0, tiled=True)]
    ppermute x0 -> x6, waiting for transfers between devices: none -> 25.6 us  [step(): return lax.ppermute(x, 'dp', pairs)]
    ppermute x0 -> x6, starting transfers between devices: none -> 18.1 us  [step(): return lax.ppermute(x, 'dp', pairs)]
    dynamic_slice x2 -> x0, local copies, waits for them, and re-layouts: 15.8 us -> none  [local(): lax.dynamic_index_in_dim(block_input.reshape(rows, n_dp, n_ten, share), t...]
    reshape x1 -> x0, local copies, waits for them, and re-layouts: 13.5 us -> none  [local(): block_input.reshape(rows, n_dp, n_ten, share)]
    ppermute x29 -> x26, starting transfers between devices: 29.1 us -> 37.1 us  [shift(): return lax.ppermute(x, axis, [(i, (i + by) % size) for i in range(size)])]
    select_n x0 -> x3, other arithmetic: none -> 6.46 us  [pick(): out = jnp.where(held, values[hop], out)]
  transfers between devices with their start and end apart: 31 -> 34, of which waited for: 14 -> 17; matrix products, arithmetic and copies ran while one was open for 18% -> 17% of each run, Pallas kernels for 4% -> 5%
where the time goes in v2:
time: 364 us; the launch traced here: 363 us
  waiting for transfers between devices  198 us (54%)
  starting transfers between devices  55.3 us (15%)
  matrix products  41.1 us (11%)
  local copies, waits for them, and re-layouts  20.5 us (6%)
  Pallas kernels  17.3 us (5%)
  other arithmetic  15.9 us (4%)
  between operations  14.6 us (4%)
    ppermute x26, waiting for transfers between devices, shift(): return lax.ppermute(x, axis, [(i, (i + by) % size) for i in range(size)])  133 us
    dot_general x13, matrix products, dot(): return lax.dot_general(a, b, dims, preferred_element_type=F32)  41.1 us
    reduce_scatter x1, waiting for transfers between devices, local(): lax.psum_scatter(value_term, 'dp', scatter_dimension=0, tiled=True)  39.4 us
    ppermute x26, starting transfers between devices, shift(): return lax.ppermute(x, axis, [(i, (i + by) % size) for i in range(size)])  37.1 us
    ppermute x6, waiting for transfers between devices, step(): return lax.ppermute(x, 'dp', pairs)  25.6 us
    ppermute x6, starting transfers between devices, step(): return lax.ppermute(x, 'dp', pairs)  18.1 us
    dynamic_slice x5, local copies, waits for them, and re-layouts, columns(): return lax.dynamic_slice_in_dim(x, start, size, 1)  10.8 us
    pallas_call x1, Pallas kernels, local(): scores(queries, saved_keys, values, attn_grad, doc_col, doc_row)  8.15 us
  transfers between devices with their start and end apart: 34, of which 17 were waited for; matrix products, arithmetic and copies ran while one was open for 17% of the time, Pallas kernels for 5%

profile of v2, /device:TPU:9, one launch (start us, length us, event | category | flops | bytes accessed | tf_op | source)
XLA Modules:
  0.0 363.0 jit_solution(18336080697262472962)
XLA Ops:
  7.2 2.1 collective-permute-start.6
  9.3 3.4 collective-permute-start.5
  12.7 23.7 %collective-permute-done.6 = bf16[768,768]{1,0:T(8,128)(2,1)S(1)} collective-permute-done((bf16[768,768]{1,0:T(8,128)(2,1)}, bf16[768,768]{1,0:T(8,128)(2,1)S(1)}, u32[]{:S(2)}, u32[]{:S(2)}) %collective-permute-start.6) | collective-permute-done | bytes 1179680 | tf_op jit(solution)/shard_map/ppermute | solution.py:124
  36.4 1.9 collective-permute-done.5
  38.3 2.6 broadcast_select_fusion
  40.9 3.2 collective-permute-start.7
  44.1 3.2 collective-permute-start.8
  47.3 2.1 constant_dynamic-slice_fusion.6
  51.1 1.1 copy-done.6
  52.2 1.1 copy-done.8
  53.3 6.7 %attend_out.1 = (bf16[512,768]{1,0:T(8,128)(2,1)S(1)}, bf16[6,512,512]{2,1,0:T(8,128)(2,1)S(1)}) custom-call(bf16[512,768]{1,0:T(8,128)(2,1)S(1)} %copy-done.4, bf16[512,768]{1,0:T(8,128)(2,1)S(1)} %copy-done.6, bf16[512,768]{1,0:T(8,128)(2,1)S(1)} %copy-done.8, s32[512,1]{1,0:T(8,128)S(1)} %copy.15.doc_col, s32[1,512]{1,0:T(1,128)S(1)} %bitcast.62), custom_call_target="tpu_custom_call" | custom-call | flops 805306368 | bytes 4718592 | tf_op jit(solution)/shard_map/attend_out/pallas_call | solution.py:177
  60.0 1.1 collective-permute-start.4
  61.2 5.5 %collective-permute-done = bf16[512,768]{1,0:T(8,128)(2,1)} collective-permute-done((bf16[512,768]{1,0:T(8,128)(2,1)}, bf16[512,768]{1,0:T(8,128)(2,1)}, u32[]{:S(2)}, u32[]{:S(2)}) %collective-permute-start) | collective-permute-done | bytes 786464 | tf_op jit(solution)/shard_map/ppermute | solution.py:117
  66.7 6.9 %collective-permute-start.1 = (bf16[512,768]{1,0:T(8,128)(2,1)}, bf16[512,768]{1,0:T(8,128)(2,1)S(1)}, u32[]{:S(2)}, u32[]{:S(2)}) collective-permute-start(bf16[512,768]{1,0:T(8,128)(2,1)} %collective-permute-done), channel_id=1, source_target_pairs={{0,8},{8,16},{16,24},{24,0},{1,9},{9,17},{17,25},{25,1},{2,10},{10... | collective-permute-start | bytes 2359304 | tf_op jit(solution)/shard_map/ppermute | solution.py:117
  73.6 1.2 select_select_fusion.1
  74.8 17.1 %collective-permute-done.9 = bf16[768,768]{1,0:T(8,128)(2,1)} collective-permute-done((bf16[768,768]{1,0:T(8,128)(2,1)}, bf16[768,768]{1,0:T(8,128)(2,1)}, u32[]{:S(2)}, u32[]{:S(2)}) %collective-permute-start.9) | collective-permute-done | bytes 1179680 | tf_op jit(solution)/shard_map/ppermute | solution.py:117
  91.9 1.9 collective-permute-start.10
  93.8 4.4 %collective-permute-start.11 = (bf16[768,768]{1,0:T(8,128)(2,1)}, bf16[768,768]{1,0:T(8,128)(2,1)}, u32[]{:S(2)}, u32[]{:S(2)}) collective-permute-start(bf16[768,768]{1,0:T(8,128)(2,1)} %collective-permute-done.8), channel_id=1, source_target_pairs={{1,0},{2,1},{3,2},{5,4},{6,5},{7,6},{9,8},{10,9},{11,10},{13,12},{... | collective-permute-start | bytes 3538952 | tf_op jit(solution)/shard_map/ppermute | solution.py:124
  99.0 9.8 %collective-permute-done.4 = bf16[512,768]{1,0:T(8,128)(2,1)} collective-permute-done((bf16[512,768]{1,0:T(8,128)(2,1)S(1)}, bf16[512,768]{1,0:T(8,128)(2,1)}, u32[]{:S(2)}, u32[]{:S(2)}) %collective-permute-start.4) | collective-permute-done | bytes 786464 | tf_op jit(solution)/shard_map/ppermute | solution.py:117
  108.8 3.0 collective-permute-start.3
  112.9 3.7 %constant_dynamic-slice_fusion.7 = bf16[512,3072]{1,0:T(8,128)(2,1)} fusion(bf16[512,6144]{1,0:T(8,128)(2,1)} %param.10, s32[]{:T(128)S(6)} %select_n.221), kind=kLoop, calls=%fused_computation.98 | loop fusion | bytes 6291460 | tf_op jit(solution)/shard_map/dynamic_slice | solution.py:120
  117.0 1.2 constant_dynamic-update-slice_fusion.11
  118.2 1.2 pad_maximum_fusion
  119.6 1.2 constant_dynamic-update-slice_fusion.9
  120.8 5.8 %collective-permute-done.3 = bf16[512,768]{1,0:T(8,128)(2,1)} collective-permute-done((bf16[512,768]{1,0:T(8,128)(2,1)}, bf16[512,768]{1,0:T(8,128)(2,1)}, u32[]{:S(2)}, u32[]{:S(2)}) %collective-permute-start.3) | collective-permute-done | bytes 786464 | tf_op jit(solution)/shard_map/ppermute | solution.py:117
  126.6 1.2 constant_dynamic-update-slice_fusion.8
  127.9 2.7 select_select_fusion
  130.5 9.2 %collective-permute-done.12 = bf16[768,768]{1,0:T(8,128)(2,1)} collective-permute-done((bf16[768,768]{1,0:T(8,128)(2,1)}, bf16[768,768]{1,0:T(8,128)(2,1)}, u32[]{:S(2)}, u32[]{:S(2)}) %collective-permute-start.12) | collective-permute-done | bytes 1179680 | tf_op jit(solution)/shard_map/ppermute | solution.py:117
  139.7 7.1 %fusion.11 = bf16[3072,768]{1,0:T(8,128)(2,1)} fusion(bf16[1024,768]{1,0:T(8,128)(2,1)S(1)} %pad_maximum_fusion, bf16[512,3072]{1,0:T(8,128)(2,1)S(1)} %constant_dynamic-update-slice_fusion.8, bf16[512,3072]{1,0:T(8,128)(2,1)S(1)} %copy-done.12), kind=kOutput, calls=%fused_computation.9 | convolution fusion | flops 4846780416 | bytes 12582912 | tf_op jit(solution)/shard_map/dot_general | solution.py:18
  146.9 2.2 constant_dynamic-slice_fusion.4
  150.1 17.5 %collective-permute-done.13 = bf16[512,768]{1,0:T(8,128)(2,1)} collective-permute-done((bf16[512,768]{1,0:T(8,128)(2,1)}, bf16[512,768]{1,0:T(8,128)(2,1)}, u32[]{:S(2)}, u32[]{:S(2)}) %collective-permute-start.13) | collective-permute-done | bytes 786464 | tf_op jit(solution)/shard_map/ppermute | solution.py:117
  167.6 2.6 collective-permute-start.14
  170.7 1.2 collective-permute-start.17
  171.9 2.3 fusion.44
  174.5 1.9 fusion.34
  176.4 2.0 fusion.38
  178.5 1.9 fusion.42
  180.4 2.3 fusion.40
  182.7 2.3 fusion.46
  185.0 11.8 %collective-permute-done.17 = bf16[768,768]{1,0:T(8,128)(2,1)S(1)} collective-permute-done((bf16[768,768]{1,0:T(8,128)(2,1)S(1)}, bf16[768,768]{1,0:T(8,128)(2,1)S(1)}, u32[]{:S(2)}, u32[]{:S(2)}) %collective-permute-start.17) | collective-permute-done | bytes 1179680 | tf_op jit(solution)/shard_map/ppermute | solution.py:117
  196.8 2.1 fusion.36
  198.9 23.2 %collective-permute-done.18 = bf16[768,768]{1,0:T(8,128)(2,1)S(1)} collective-permute-done((bf16[768,768]{1,0:T(8,128)(2,1)S(1)}, bf16[768,768]{1,0:T(8,128)(2,1)S(1)}, u32[]{:S(2)}, u32[]{:S(2)}) %collective-permute-start.18) | collective-permute-done | bytes 1179680 | tf_op jit(solution)/shard_map/ppermute | solution.py:117
  222.1 2.5 add_convert_fusion.g
  224.6 2.4 value_grad.1
  227.0 1.3 collective-permute-start.19
  229.0 1.2 constant_dynamic-update-slice_fusion.7
  230.5 13.3 %collective-permute-done.19 = bf16[512,768]{1,0:T(8,128)(2,1)S(1)} collective-permute-done((bf16[512,768]{1,0:T(8,128)(2,1)S(1)}, bf16[512,768]{1,0:T(8,128)(2,1)S(1)}, u32[]{:S(2)}, u32[]{:S(2)}) %collective-permute-start.19) | collective-permute-done | bytes 786464 | tf_op jit(solution)/shard_map/ppermute | solution.py:117
  243.8 7.0 %fusion.8 = bf16[3072,768]{1,0:T(8,128)(2,1)} fusion(bf16[512,3072]{1,0:T(8,128)(2,1)S(1)} %constant_dynamic-update-slice_fusion.4, bf16[512,3072]{1,0:T(8,128)(2,1)S(1)} %constant_dynamic-slice_fusion.5, bf16[512,768]{1,0:T(8,128)(2,1)S(1)} %collective-permute-done.19, bf16[512,768]{1,0:T(8,128)(2,1)S(1)} %value_grad.1), kind=kOutput, calls=%fused_computation.8 | convolution fusion | flops 4849926144 | bytes 12582912 | tf_op jit(solution)/shard_map/dot_general | solution.py:18
  251.0 2.6 constant_dynamic-slice_fusion.3
  254.7 4.8 %collective-permute-start.20 = (bf16[512,128]{1,0:T(8,128)(2,1)S(1)}, bf16[512,128]{1,0:T(8,128)(2,1)}, u32[]{:S(2)}, u32[]{:S(2)}) collective-permute-start(bf16[512,128]{1,0:T(8,128)(2,1)S(1)} %get-tuple-element.54), channel_id=1, source_target_pairs={{0,8},{8,16},{16,24},{24,0},{1,9},{9,17},{17,25},{25,1},{2,10},{10... | collective-permute-start | bytes 393224 | tf_op jit(solution)/shard_map/ppermute | solution.py:117
  259.8 6.3 %fusion.31 = f32[128,768]{1,0:T(8,128)} fusion(bf16[512,768]{1,0:T(8,128)(2,1)S(1)} %value_grad.1, bf16[512,6144]{1,0:T(8,128)(2,1)} %param.9, bf16[1,6144,128]{2,1,0:T(8,128)(2,1)S(1)} %copy-done), kind=kOutput, calls=%fused_computation.31 | convolution fusion | flops 906035200 | bytes 9043968 | tf_op jit(solution)/shard_map/dot_general | solution.py:18
  267.4 2.9 collective-permute-start.30
  270.3 2.4 fusion.17
  272.9 3.3 collective-permute-start.24
  276.2 8.1 %score_grads.1 = (bf16[512,768]{1,0:T(8,128)(2,1)}, bf16[512,768]{1,0:T(8,128)(2,1)}) custom-call(bf16[512,768]{1,0:T(8,128)(2,1)S(1)} %copy-done.5, bf16[512,768]{1,0:T(8,128)(2,1)S(1)} %copy-done.7, bf16[512,768]{1,0:T(8,128)(2,1)S(1)} %copy-done.9, bf16[512,768]{1,0:T(8,128)(2,1)S(1)} %add_convert_fusion.g, s32[512,1]{1,0:T(8,128)S(1)} %copy.15.doc_col, ...), custom_call_target="tpu_custom_call" | custom-call | flops 1610612736 | bytes 5505024 | tf_op jit(solution)/shard_map/score_grads/pallas_call | solution.py:195
  284.4 1.2 collective-permute-start.31
  285.5 11.0 %collective-permute-done.24 = bf16[384,128]{1,0:T(8,128)(2,1)S(1)} collective-permute-done((bf16[384,128]{1,0:T(8,128)(2,1)S(1)}, bf16[384,128]{1,0:T(8,128)(2,1)S(1)}, u32[]{:S(2)}, u32[]{:S(2)}) %collective-permute-start.24) | collective-permute-done | bytes 98336 | tf_op jit(solution)/shard_map/ppermute | solution.py:117
  297.5 1.4 collective-permute-start.26
  299.0 1.4 collective-permute-start.27
  300.4 1.6 fusion.58
  302.9 6.6 %collective-permute-done.27 = f32[384,128]{1,0:T(8,128)S(1)} collective-permute-done((f32[384,128]{1,0:T(8,128)S(1)}, f32[384,128]{1,0:T(8,128)S(1)}, u32[]{:S(2)}, u32[]{:S(2)}) %collective-permute-start.27) | collective-permute-done | bytes 196640 | tf_op jit(solution)/shard_map/ppermute | solution.py:117
  311.1 2.8 convert_multiply_fusion.1
  313.9 39.4 %reduce-scatter.5.cloned.1.call-done = bf16[768,768]{1,0:T(8,128)(2,1)} async-done(((bf16[3072,768]{1,0:T(8,128)(2,1)}), bf16[768,768]{1,0:T(8,128)(2,1)}) %reduce-scatter.5.cloned.1.call-update) | async-done | bytes 1179664 | tf_op jit(solution)/shard_map/reduce_scatter | solution.py:194
  353.4 2.8 convert_multiply_fusion
  (92 shorter events, 13.5 us)
Async XLA Ops:
  7.2 252.7 %copy-start = (bf16[1,6144,128]{2,1,0:T(8,128)(2,1)S(1)}, bf16[1,6144,128]{2,1,0:T(8,128)(2,1)}, u32[]{:S(2)}) copy-start(bf16[1,6144,128]{2,1,0:T(8,128)(2,1)} %param.16) | copy-start | bytes 4718596
  7.2 303.9 %reduce-scatter.3.cloned.1.call-start = ((), (), s32[]{:S(2)}) async-start(), calls=%async_computation.2 | async-start | bytes 5898240 | tf_op jit(solution)/shard_map/reduce_scatter | solution.py:183
  7.2 29.2 %collective-permute-start.6 = (bf16[768,768]{1,0:T(8,128)(2,1)}, bf16[768,768]{1,0:T(8,128)(2,1)S(1)}, u32[]{:S(2)}, u32[]{:S(2)}) collective-permute-start(bf16[768,768]{1,0:T(8,128)(2,1)} %param.15), channel_id=1, source_target_pairs={{1,0},{2,1},{3,2},{5,4},{6,5},{7,6},{9,8},{10,9},{11,10},{13,12},{... | collective-permute-start | bytes 3538952 | tf_op jit(solution)/shard_map/ppermute | solution.py:124
  9.3 29.0 %collective-permute-start.5 = (bf16[768,768]{1,0:T(8,128)(2,1)}, bf16[768,768]{1,0:T(8,128)(2,1)}, u32[]{:S(2)}, u32[]{:S(2)}) collective-permute-start(bf16[768,768]{1,0:T(8,128)(2,1)} %param.15), channel_id=1, source_target_pairs={{0,1},{1,2},{2,3},{4,5},{5,6},{6,7},{8,9},{9,10},{10,11},{12,13},{... | collective-permute-start | bytes 3538952 | tf_op jit(solution)/shard_map/ppermute | solution.py:124
  36.4 1.9 copy-start.10
  40.9 10.0 %copy-start.3 = (s32[512]{0:T(512)S(1)}, s32[512]{0:T(512)}, u32[]{:S(2)}) copy-start(s32[512]{0:T(512)} %param.14) | copy-start | bytes 6148
  40.9 10.1 %copy-start.4 = (bf16[512,768]{1,0:T(8,128)(2,1)S(1)}, bf16[512,768]{1,0:T(8,128)(2,1)}, u32[]{:S(2)}) copy-start(bf16[512,768]{1,0:T(8,128)(2,1)} %q.3) | copy-start | bytes 2359300
  40.9 32.7 %collective-permute-start.7 = (bf16[768,768]{1,0:T(8,128)(2,1)}, bf16[768,768]{1,0:T(8,128)(2,1)}, u32[]{:S(2)}, u32[]{:S(2)}) collective-permute-start(bf16[768,768]{1,0:T(8,128)(2,1)} %collective-permute-done.5), channel_id=1, source_target_pairs={{0,1},{1,2},{2,3},{4,5},{5,6},{6,7},{8,9},{9,10},{10,11},{12,13},{... | collective-permute-start | bytes 3538952 | tf_op jit(solution)/shard_map/ppermute | solution.py:124
  44.1 29.5 %collective-permute-start.8 = (bf16[768,768]{1,0:T(8,128)(2,1)}, bf16[768,768]{1,0:T(8,128)(2,1)}, u32[]{:S(2)}, u32[]{:S(2)}) collective-permute-start(bf16[768,768]{1,0:T(8,128)(2,1)} %copy-done.10), channel_id=1, source_target_pairs={{1,0},{2,1},{3,2},{5,4},{6,5},{7,6},{9,8},{10,9},{11,10},{13,12},{... | collective-permute-start | bytes 3538952 | tf_op jit(solution)/shard_map/ppermute | solution.py:124
  49.4 17.2 %collective-permute-start = (bf16[512,768]{1,0:T(8,128)(2,1)}, bf16[512,768]{1,0:T(8,128)(2,1)}, u32[]{:S(2)}, u32[]{:S(2)}) collective-permute-start(bf16[512,768]{1,0:T(8,128)(2,1)} %constant_dynamic-slice_fusion.6), channel_id=1, source_target_pairs={{0,4},{4,0},{1,5},{5,1},{2,6},{6,2},{3,7},{7,3},{8,12},{12,8},{9,1... | collective-permute-start | bytes 2359304 | tf_op jit(solution)/shard_map/ppermute | solution.py:117
  50.5 41.4 %collective-permute-start.9 = (bf16[768,768]{1,0:T(8,128)(2,1)}, bf16[768,768]{1,0:T(8,128)(2,1)}, u32[]{:S(2)}, u32[]{:S(2)}) collective-permute-start(bf16[768,768]{1,0:T(8,128)(2,1)} %param.15), channel_id=1, source_target_pairs={{0,4},{4,0},{1,5},{5,1},{2,6},{6,2},{3,7},{7,3},{8,12},{12,8},{9,1... | collective-permute-start | bytes 3538952 | tf_op jit(solution)/shard_map/ppermute | solution.py:117
  51.0 1.1 copy-start.6
  52.2 1.1 copy-start.8
  53.3 20.3 %copy-start.11 = (bf16[768,768]{1,0:T(8,128)(2,1)S(1)}, bf16[768,768]{1,0:T(8,128)(2,1)}, u32[]{:S(2)}) copy-start(bf16[768,768]{1,0:T(8,128)(2,1)} %copy-done.10) | copy-start | bytes 3538948
  60.0 14.8 %copy-start.1 = (bf16[6,512,512]{2,1,0:T(8,128)(2,1)}, bf16[6,512,512]{2,1,0:T(8,128)(2,1)S(1)}, u32[]{:S(2)}) copy-start(bf16[6,512,512]{2,1,0:T(8,128)(2,1)S(1)} %get-tuple-element.33.half) | copy-start | bytes 9437188
  60.0 48.7 %collective-permute-start.4 = (bf16[512,768]{1,0:T(8,128)(2,1)S(1)}, bf16[512,768]{1,0:T(8,128)(2,1)}, u32[]{:S(2)}, u32[]{:S(2)}) collective-permute-start(bf16[512,768]{1,0:T(8,128)(2,1)S(1)} %get-tuple-element.24), channel_id=1, source_target_pairs={{0,4},{4,0},{1,5},{5,1},{2,6},{6,2},{3,7},{7,3},{8,12},{12,8},{9,1... | collective-permute-start | bytes 2359304 | tf_op jit(solution)/shard_map/ppermute | solution.py:117
  66.7 45.2 %collective-permute-start.1 = (bf16[512,768]{1,0:T(8,128)(2,1)}, bf16[512,768]{1,0:T(8,128)(2,1)S(1)}, u32[]{:S(2)}, u32[]{:S(2)}) collective-permute-start(bf16[512,768]{1,0:T(8,128)(2,1)} %collective-permute-done), channel_id=1, source_target_pairs={{0,8},{8,16},{16,24},{24,0},{1,9},{9,17},{17,25},{25,1},{2,10},{10... | collective-permute-start | bytes 2359304 | tf_op jit(solution)/shard_map/ppermute | solution.py:117
  91.9 35.9 %collective-permute-start.10 = (bf16[768,768]{1,0:T(8,128)(2,1)}, bf16[768,768]{1,0:T(8,128)(2,1)}, u32[]{:S(2)}, u32[]{:S(2)}) collective-permute-start(bf16[768,768]{1,0:T(8,128)(2,1)} %collective-permute-done.7), channel_id=1, source_target_pairs={{0,1},{1,2},{2,3},{4,5},{5,6},{6,7},{8,9},{9,10},{10,11},{12,13},{... | collective-permute-start | bytes 3538952 | tf_op jit(solution)/shard_map/ppermute | solution.py:124
  93.8 34.0 %collective-permute-start.11 = (bf16[768,768]{1,0:T(8,128)(2,1)}, bf16[768,768]{1,0:T(8,128)(2,1)}, u32[]{:S(2)}, u32[]{:S(2)}) collective-permute-start(bf16[768,768]{1,0:T(8,128)(2,1)} %collective-permute-done.8), channel_id=1, source_target_pairs={{1,0},{2,1},{3,2},{5,4},{6,5},{7,6},{9,8},{10,9},{11,10},{13,12},{... | collective-permute-start | bytes 3538952 | tf_op jit(solution)/shard_map/ppermute | solution.py:124
  98.2 21.4 %collective-permute-start.2 = (bf16[512,768]{1,0:T(8,128)(2,1)}, bf16[512,768]{1,0:T(8,128)(2,1)}, u32[]{:S(2)}, u32[]{:S(2)}) collective-permute-start(bf16[512,768]{1,0:T(8,128)(2,1)} %collective-permute-done), channel_id=1, source_target_pairs={{0,16},{8,24},{16,0},{24,8},{1,17},{9,25},{17,1},{25,9},{2,18},{10... | collective-permute-start | bytes 2359304 | tf_op jit(solution)/shard_map/ppermute | solution.py:117
  108.8 17.8 %collective-permute-start.3 = (bf16[512,768]{1,0:T(8,128)(2,1)}, bf16[512,768]{1,0:T(8,128)(2,1)}, u32[]{:S(2)}, u32[]{:S(2)}) collective-permute-start(bf16[512,768]{1,0:T(8,128)(2,1)} %collective-permute-done), channel_id=1, source_target_pairs={{0,24},{8,0},{16,8},{24,16},{1,25},{9,1},{17,9},{25,17},{2,26},{10... | collective-permute-start | bytes 2359304 | tf_op jit(solution)/shard_map/ppermute | solution.py:117
  111.8 27.9 %collective-permute-start.12 = (bf16[768,768]{1,0:T(8,128)(2,1)}, bf16[768,768]{1,0:T(8,128)(2,1)}, u32[]{:S(2)}, u32[]{:S(2)}) collective-permute-start(bf16[768,768]{1,0:T(8,128)(2,1)} %broadcast_select_fusion), channel_id=1, source_target_pairs={{0,4},{4,0},{1,5},{5,1},{2,6},{6,2},{3,7},{7,3},{8,12},{12,8},{9,1... | collective-permute-start | bytes 3538952 | tf_op jit(solution)/shard_map/ppermute | solution.py:117
  127.8 11.9 %copy-start.12 = (bf16[512,3072]{1,0:T(8,128)(2,1)S(1)}, bf16[512,3072]{1,0:T(8,128)(2,1)}, u32[]{:S(2)}) copy-start(bf16[512,3072]{1,0:T(8,128)(2,1)} %constant_dynamic-slice_fusion.7) | copy-start | bytes 9437188
  146.8 23.9 %copy-start.13 = (bf16[768,768]{1,0:T(8,128)(2,1)S(1)}, bf16[768,768]{1,0:T(8,128)(2,1)}, u32[]{:S(2)}) copy-start(bf16[768,768]{1,0:T(8,128)(2,1)} %select_select_fusion.1) | copy-start | bytes 3538948
  146.8 206.5 %reduce-scatter.5.cloned.1.call-start = ((), (), s32[]{:S(2)}) async-start(), calls=%async_computation.3 | async-start | bytes 5898240 | tf_op jit(solution)/shard_map/reduce_scatter | solution.py:194
  149.0 18.6 %collective-permute-start.13 = (bf16[512,768]{1,0:T(8,128)(2,1)}, bf16[512,768]{1,0:T(8,128)(2,1)}, u32[]{:S(2)}, u32[]{:S(2)}) collective-permute-start(bf16[512,768]{1,0:T(8,128)(2,1)} %constant_dynamic-slice_fusion.4), channel_id=1, source_target_pairs={{0,4},{4,0},{1,5},{5,1},{2,6},{6,2},{3,7},{7,3},{8,12},{12,8},{9,1... | collective-permute-start | bytes 2359304 | tf_op jit(solution)/shard_map/ppermute | solution.py:117
  150.1 24.1 %copy-start.14 = (bf16[768,768]{1,0:T(8,128)(2,1)S(1)}, bf16[768,768]{1,0:T(8,128)(2,1)}, u32[]{:S(2)}) copy-start(bf16[768,768]{1,0:T(8,128)(2,1)} %select_select_fusion) | copy-start | bytes 3538948
  167.6 62.6 %collective-permute-start.14 = (bf16[512,768]{1,0:T(8,128)(2,1)}, bf16[512,768]{1,0:T(8,128)(2,1)S(1)}, u32[]{:S(2)}, u32[]{:S(2)}) collective-permute-start(bf16[512,768]{1,0:T(8,128)(2,1)} %collective-permute-done.13), channel_id=1, source_target_pairs={{0,8},{8,16},{16,24},{24,0},{1,9},{9,17},{17,25},{25,1},{2,10},{10... | collective-permute-start | bytes 2359304 | tf_op jit(solution)/shard_map/ppermute | solution.py:117
  170.3 60.1 %collective-permute-start.15 = (bf16[512,768]{1,0:T(8,128)(2,1)}, bf16[512,768]{1,0:T(8,128)(2,1)S(1)}, u32[]{:S(2)}, u32[]{:S(2)}) collective-permute-start(bf16[512,768]{1,0:T(8,128)(2,1)} %collective-permute-done.13), channel_id=1, source_target_pairs={{0,16},{8,24},{16,0},{24,8},{1,17},{9,25},{17,1},{25,9},{2,18},{10... | collective-permute-start | bytes 2359304 | tf_op jit(solution)/shard_map/ppermute | solution.py:117
  170.7 59.8 %collective-permute-start.16 = (bf16[512,768]{1,0:T(8,128)(2,1)}, bf16[512,768]{1,0:T(8,128)(2,1)S(1)}, u32[]{:S(2)}, u32[]{:S(2)}) collective-permute-start(bf16[512,768]{1,0:T(8,128)(2,1)} %collective-permute-done.13), channel_id=1, source_target_pairs={{0,24},{8,0},{16,8},{24,16},{1,25},{9,1},{17,9},{25,17},{2,26},{10... | collective-permute-start | bytes 2359304 | tf_op jit(solution)/shard_map/ppermute | solution.py:117
  170.7 26.1 %collective-permute-start.17 = (bf16[768,768]{1,0:T(8,128)(2,1)S(1)}, bf16[768,768]{1,0:T(8,128)(2,1)S(1)}, u32[]{:S(2)}, u32[]{:S(2)}) collective-permute-start(bf16[768,768]{1,0:T(8,128)(2,1)S(1)} %copy-done.13), channel_id=1, source_target_pairs={{0,4},{4,0},{1,5},{5,1},{2,6},{6,2},{3,7},{7,3},{8,12},{12,8},{9,1... | collective-permute-start | bytes 3538952 | tf_op jit(solution)/shard_map/ppermute | solution.py:117
  174.2 47.9 %collective-permute-start.18 = (bf16[768,768]{1,0:T(8,128)(2,1)S(1)}, bf16[768,768]{1,0:T(8,128)(2,1)S(1)}, u32[]{:S(2)}, u32[]{:S(2)}) collective-permute-start(bf16[768,768]{1,0:T(8,128)(2,1)S(1)} %copy-done.14), channel_id=1, source_target_pairs={{0,4},{4,0},{1,5},{5,1},{2,6},{6,2},{3,7},{7,3},{8,12},{12,8},{9,1... | collective-permute-start | bytes 3538952 | tf_op jit(solution)/shard_map/ppermute | solution.py:117
  176.4 2.0 copy-start.15
  196.8 31.5 %slice-start = ((s8[6291456]{0:T(1024)(128)(4,1)}), s8[4194304]{0:T(1024)(128)(4,1)S(1)}, s32[]{:S(2)}) async-start(s8[6291456]{0:T(1024)(128)(4,1)} %bitcast.64), calls=%async_computation.4 | async-start | bytes 8388608
  198.9 29.4 %slice-start.1 = ((s8[6291456]{0:T(1024)(128)(4,1)}), s8[2097152]{0:T(1024)(128)(4,1)S(1)}, s32[]{:S(2)}) async-start(s8[6291456]{0:T(1024)(128)(4,1)} %bitcast.64), calls=%async_computation.5 | async-start | bytes 4194304
  222.1 2.5 copy-start.2
  227.0 16.9 %collective-permute-start.19 = (bf16[512,768]{1,0:T(8,128)(2,1)S(1)}, bf16[512,768]{1,0:T(8,128)(2,1)S(1)}, u32[]{:S(2)}, u32[]{:S(2)}) collective-permute-start(bf16[512,768]{1,0:T(8,128)(2,1)S(1)} %value_grad.1), channel_id=1, source_target_pairs={{0,4},{4,0},{1,5},{5,1},{2,6},{6,2},{3,7},{7,3},{8,12},{12,8},{9,1... | collective-permute-start | bytes 2359304 | tf_op jit(solution)/shard_map/ppermute | solution.py:117
  251.0 2.6 copy-start.16
  254.7 15.6 %collective-permute-start.20 = (bf16[512,128]{1,0:T(8,128)(2,1)S(1)}, bf16[512,128]{1,0:T(8,128)(2,1)}, u32[]{:S(2)}, u32[]{:S(2)}) collective-permute-start(bf16[512,128]{1,0:T(8,128)(2,1)S(1)} %get-tuple-element.54), channel_id=1, source_target_pairs={{0,8},{8,16},{16,24},{24,0},{1,9},{9,17},{17,25},{25,1},{2,10},{10... | collective-permute-start | bytes 393224 | tf_op jit(solution)/shard_map/ppermute | solution.py:117
  259.4 10.9 %collective-permute-start.21 = (bf16[512,128]{1,0:T(8,128)(2,1)S(1)}, bf16[512,128]{1,0:T(8,128)(2,1)}, u32[]{:S(2)}, u32[]{:S(2)}) collective-permute-start(bf16[512,128]{1,0:T(8,128)(2,1)S(1)} %get-tuple-element.54), channel_id=1, source_target_pairs={{0,16},{8,24},{16,0},{24,8},{1,17},{9,25},{17,1},{25,9},{2,18},{10... | collective-permute-start | bytes 393224 | tf_op jit(solution)/shard_map/ppermute | solution.py:117
  259.4 10.9 %collective-permute-start.22 = (bf16[512,128]{1,0:T(8,128)(2,1)S(1)}, bf16[512,128]{1,0:T(8,128)(2,1)}, u32[]{:S(2)}, u32[]{:S(2)}) collective-permute-start(bf16[512,128]{1,0:T(8,128)(2,1)S(1)} %get-tuple-element.54), channel_id=1, source_target_pairs={{0,24},{8,0},{16,8},{24,16},{1,25},{9,1},{17,9},{25,17},{2,26},{10... | collective-permute-start | bytes 393224 | tf_op jit(solution)/shard_map/ppermute | solution.py:117
  267.1 33.2 %collective-permute-start.29 = (bf16[32,768]{1,0:T(8,128)(2,1)S(1)}, bf16[32,768]{1,0:T(8,128)(2,1)S(1)}, u32[]{:S(2)}, u32[]{:S(2)}) collective-permute-start(bf16[32,768]{1,0:T(8,128)(2,1)S(1)} %get-tuple-element.51), channel_id=1, source_target_pairs={{0,1},{1,2},{2,3},{3,0},{4,5},{5,6},{6,7},{7,4},{8,9},{9,10},{10,1... | collective-permute-start | bytes 147464 | tf_op jit(solution)/shard_map/ppermute | solution.py:117
  267.4 32.9 %collective-permute-start.30 = (bf16[32,768]{1,0:T(8,128)(2,1)S(1)}, bf16[32,768]{1,0:T(8,128)(2,1)S(1)}, u32[]{:S(2)}, u32[]{:S(2)}) collective-permute-start(bf16[32,768]{1,0:T(8,128)(2,1)S(1)} %get-tuple-element.53), channel_id=1, source_target_pairs={{0,2},{1,3},{2,0},{3,1},{4,6},{5,7},{6,4},{7,5},{8,10},{9,11},{10,... | collective-permute-start | bytes 147464 | tf_op jit(solution)/shard_map/ppermute | solution.py:117
  270.3 5.9 %copy-start.5 = (bf16[512,768]{1,0:T(8,128)(2,1)S(1)}, bf16[512,768]{1,0:T(8,128)(2,1)}, u32[]{:S(2)}) copy-start(bf16[512,768]{1,0:T(8,128)(2,1)} %q.3) | copy-start | bytes 2359300
  270.3 5.9 %copy-start.7 = (bf16[512,768]{1,0:T(8,128)(2,1)S(1)}, bf16[512,768]{1,0:T(8,128)(2,1)}, u32[]{:S(2)}) copy-start(bf16[512,768]{1,0:T(8,128)(2,1)} %k.3) | copy-start | bytes 2359300
  270.3 5.9 %copy-start.9 = (bf16[512,768]{1,0:T(8,128)(2,1)S(1)}, bf16[512,768]{1,0:T(8,128)(2,1)}, u32[]{:S(2)}) copy-start(bf16[512,768]{1,0:T(8,128)(2,1)} %v.3) | copy-start | bytes 2359300
  272.8 11.6 %collective-permute-start.23 = (bf16[384,128]{1,0:T(8,128)(2,1)S(1)}, bf16[384,128]{1,0:T(8,128)(2,1)S(1)}, u32[]{:S(2)}, u32[]{:S(2)}) collective-permute-start(bf16[384,128]{1,0:T(8,128)(2,1)S(1)} %get-tuple-element.48), channel_id=1, source_target_pairs={{0,1},{1,2},{2,3},{3,0},{4,5},{5,6},{6,7},{7,4},{8,9},{9,10},{10,1... | collective-permute-start | bytes 294920 | tf_op jit(solution)/shard_map/ppermute | solution.py:117
  272.9 23.6 %collective-permute-start.24 = (bf16[384,128]{1,0:T(8,128)(2,1)S(1)}, bf16[384,128]{1,0:T(8,128)(2,1)S(1)}, u32[]{:S(2)}, u32[]{:S(2)}) collective-permute-start(bf16[384,128]{1,0:T(8,128)(2,1)S(1)} %get-tuple-element.50), channel_id=1, source_target_pairs={{0,2},{1,3},{2,0},{3,1},{4,6},{5,7},{6,4},{7,5},{8,10},{9,11},{10,... | collective-permute-start | bytes 294920 | tf_op jit(solution)/shard_map/ppermute | solution.py:117
  276.2 21.2 %collective-permute-start.25 = (bf16[384,128]{1,0:T(8,128)(2,1)S(1)}, bf16[384,128]{1,0:T(8,128)(2,1)S(1)}, u32[]{:S(2)}, u32[]{:S(2)}) collective-permute-start(bf16[384,128]{1,0:T(8,128)(2,1)S(1)} %get-tuple-element.49), channel_id=1, source_target_pairs={{0,3},{1,0},{2,1},{3,2},{4,7},{5,4},{6,5},{7,6},{8,11},{9,8},{10,9... | collective-permute-start | bytes 294920 | tf_op jit(solution)/shard_map/ppermute | solution.py:117
  284.4 16.0 %collective-permute-start.31 = (bf16[32,768]{1,0:T(8,128)(2,1)S(1)}, bf16[32,768]{1,0:T(8,128)(2,1)S(1)}, u32[]{:S(2)}, u32[]{:S(2)}) collective-permute-start(bf16[32,768]{1,0:T(8,128)(2,1)S(1)} %get-tuple-element.52), channel_id=1, source_target_pairs={{0,3},{1,0},{2,1},{3,2},{4,7},{5,4},{6,5},{7,6},{8,11},{9,8},{10,9... | collective-permute-start | bytes 147464 | tf_op jit(solution)/shard_map/ppermute | solution.py:117
  297.5 5.4 %collective-permute-start.26 = (f32[384,128]{1,0:T(8,128)S(1)}, f32[384,128]{1,0:T(8,128)S(1)}, u32[]{:S(2)}, u32[]{:S(2)}) collective-permute-start(f32[384,128]{1,0:T(8,128)S(1)} %get-tuple-element.43), channel_id=1, source_target_pairs={{0,8},{8,16},{16,24},{24,0},{1,9},{9,17},{17,25},{25,1},{2,10},{10... | collective-permute-start | bytes 589832 | tf_op jit(solution)/shard_map/ppermute | solution.py:117
  299.0 10.5 %collective-permute-start.27 = (f32[384,128]{1,0:T(8,128)S(1)}, f32[384,128]{1,0:T(8,128)S(1)}, u32[]{:S(2)}, u32[]{:S(2)}) collective-permute-start(f32[384,128]{1,0:T(8,128)S(1)} %get-tuple-element.43), channel_id=1, source_target_pairs={{0,16},{8,24},{16,0},{24,8},{1,17},{9,25},{17,1},{25,9},{2,18},{10... | collective-permute-start | bytes 589832 | tf_op jit(solution)/shard_map/ppermute | solution.py:117
  301.9 8.2 %collective-permute-start.28 = (f32[384,128]{1,0:T(8,128)S(1)}, f32[384,128]{1,0:T(8,128)S(1)}, u32[]{:S(2)}, u32[]{:S(2)}) collective-permute-start(f32[384,128]{1,0:T(8,128)S(1)} %get-tuple-element.43), channel_id=1, source_target_pairs={{0,24},{8,0},{16,8},{24,16},{1,25},{9,1},{17,9},{25,17},{2,26},{10... | collective-permute-start | bytes 589832 | tf_op jit(solution)/shard_map/ppermute | solution.py:117
Sparse Core Ops, SparseCore 0:
  146.9 86.4 reduce-scatter.2
  251.0 102.3 reduce-scatter.4

commit v3 on v2

--- a/solution.py
+++ b/solution.py
@@ -147,12 +147,11 @@
         below, above = step(below, 1), step(above, -1)
         arrivals[k], arrivals[-k] = below, above
         choices = [order[d][k - 1] for d in range(n_dp)]
-        sent = slots[k - 2][2] if k > 1 else []
+        sent = slots[k - 1][2]
         here, below, above, sent = lax.optimization_barrier(
             (pick(choices, arrivals), below, above, sent)
         )
-        if k > 1:
-            slots[k - 2] = (*slots[k - 2][:2], sent)
+        slots[k - 1] = (*slots[k - 1][:2], sent)
         hops = {hop: jnp.int32(hop) for hop in arrivals}
         slots.append((dp - pick(choices, hops), here, forwards(here)))
 

time: 364 us -> 345 us (0.948)
  waiting for transfers between devices: 198 us -> 178 us
    ppermute x26, waiting for transfers between devices: 133 us -> 112 us  [shift(): return lax.ppermute(x, axis, [(i, (i + by) % size) for i in range(size)])]
  transfers between devices with their start and end apart: 34 -> 34, of which waited for: 17 -> 15; matrix products, arithmetic and copies ran while one was open for 17% -> 19% of each run, Pallas kernels for 5% -> 5%
where the time goes in v3:
time: 345 us; the launch traced here: 344 us
  waiting for transfers between devices  178 us (52%)
  starting transfers between devices  58.5 us (17%)
  matrix products  40.7 us (12%)
  local copies, waits for them, and re-layouts  20.4 us (6%)
  Pallas kernels  17.3 us (5%)
  other arithmetic  14.8 us (4%)
  between operations  14.6 us (4%)
    ppermute x26, waiting for transfers between devices, shift(): return lax.ppermute(x, axis, [(i, (i + by) % size) for i in range(size)])  112 us
    reduce_scatter x1, waiting for transfers between devices, local(): lax.psum_scatter(value_term, 'dp', scatter_dimension=0, tiled=True)  41.2 us
    dot_general x13, matrix products, dot(): return lax.dot_general(a, b, dims, preferred_element_type=F32)  40.7 us
    ppermute x26, starting transfers between devices, shift(): return lax.ppermute(x, axis, [(i, (i + by) % size) for i in range(size)])  40.3 us
    ppermute x6, waiting for transfers between devices, step(): return lax.ppermute(x, 'dp', pairs)  24.4 us
    ppermute x6, starting transfers between devices, step(): return lax.ppermute(x, 'dp', pairs)  18.1 us
    dynamic_slice x5, local copies, waits for them, and re-layouts, columns(): return lax.dynamic_slice_in_dim(x, start, size, 1)  10.7 us
    pallas_call x1, Pallas kernels, local(): scores(queries, saved_keys, values, attn_grad, doc_col, doc_row)  8.15 us
  transfers between devices with their start and end apart: 34, of which 15 were waited for; matrix products, arithmetic and copies ran while one was open for 19% of the time, Pallas kernels for 5%

profile of v3, /device:TPU:9, one launch (start us, length us, event | category | flops | bytes accessed | tf_op | source)
XLA Modules:
  0.0 343.8 jit_solution(16170883186559405297)
XLA Ops:
  7.2 2.1 collective-permute-start.6
  9.3 3.4 collective-permute-start.5
  12.7 1.3 collective-permute-start.7
  14.0 22.4 %collective-permute-done.6 = bf16[768,768]{1,0:T(8,128)(2,1)S(1)} collective-permute-done((bf16[768,768]{1,0:T(8,128)(2,1)}, bf16[768,768]{1,0:T(8,128)(2,1)S(1)}, u32[]{:S(2)}, u32[]{:S(2)}) %collective-permute-start.6) | collective-permute-done | bytes 1179680 | tf_op jit(solution)/shard_map/ppermute | solution.py:124
  36.4 1.9 collective-permute-done.5
  38.3 2.5 broadcast_select_fusion
  40.8 3.2 collective-permute-start.8
  44.0 3.2 collective-permute-start.9
  47.2 2.1 constant_dynamic-slice_fusion.6
  51.0 1.1 copy-done.6
  52.1 1.1 copy-done.8
  53.2 6.7 %attend_out.1 = (bf16[512,768]{1,0:T(8,128)(2,1)S(1)}, bf16[6,512,512]{2,1,0:T(8,128)(2,1)S(1)}) custom-call(bf16[512,768]{1,0:T(8,128)(2,1)S(1)} %copy-done.4, bf16[512,768]{1,0:T(8,128)(2,1)S(1)} %copy-done.6, bf16[512,768]{1,0:T(8,128)(2,1)S(1)} %copy-done.8, s32[512,1]{1,0:T(8,128)S(1)} %copy.15.doc_col, s32[1,512]{1,0:T(1,128)S(1)} %bitcast.62), custom_call_target="tpu_custom_call" | custom-call | flops 805306368 | bytes 4718592 | tf_op jit(solution)/shard_map/attend_out/pallas_call | solution.py:176
  60.0 1.1 collective-permute-start.4
  61.1 5.5 %collective-permute-done = bf16[512,768]{1,0:T(8,128)(2,1)} collective-permute-done((bf16[512,768]{1,0:T(8,128)(2,1)}, bf16[512,768]{1,0:T(8,128)(2,1)}, u32[]{:S(2)}, u32[]{:S(2)}) %collective-permute-start) | collective-permute-done | bytes 786464 | tf_op jit(solution)/shard_map/ppermute | solution.py:117
  66.6 6.9 %collective-permute-start.1 = (bf16[512,768]{1,0:T(8,128)(2,1)}, bf16[512,768]{1,0:T(8,128)(2,1)S(1)}, u32[]{:S(2)}, u32[]{:S(2)}) collective-permute-start(bf16[512,768]{1,0:T(8,128)(2,1)} %collective-permute-done), channel_id=1, source_target_pairs={{0,8},{8,16},{16,24},{24,0},{1,9},{9,17},{17,25},{25,1},{2,10},{10... | collective-permute-start | bytes 2359304 | tf_op jit(solution)/shard_map/ppermute | solution.py:117
  73.5 1.2 select_select_fusion.1
  74.7 17.1 %collective-permute-done.10 = bf16[768,768]{1,0:T(8,128)(2,1)} collective-permute-done((bf16[768,768]{1,0:T(8,128)(2,1)}, bf16[768,768]{1,0:T(8,128)(2,1)}, u32[]{:S(2)}, u32[]{:S(2)}) %collective-permute-start.10) | collective-permute-done | bytes 1179680 | tf_op jit(solution)/shard_map/ppermute | solution.py:117
  91.8 1.9 collective-permute-start.11
  93.8 4.4 %collective-permute-start.12 = (bf16[768,768]{1,0:T(8,128)(2,1)}, bf16[768,768]{1,0:T(8,128)(2,1)}, u32[]{:S(2)}, u32[]{:S(2)}) collective-permute-start(bf16[768,768]{1,0:T(8,128)(2,1)} %collective-permute-done.9), channel_id=1, source_target_pairs={{1,0},{2,1},{3,2},{5,4},{6,5},{7,6},{9,8},{10,9},{11,10},{13,12},{... | collective-permute-start | bytes 3538952 | tf_op jit(solution)/shard_map/ppermute | solution.py:124
  98.9 9.8 %collective-permute-done.4 = bf16[512,768]{1,0:T(8,128)(2,1)} collective-permute-done((bf16[512,768]{1,0:T(8,128)(2,1)S(1)}, bf16[512,768]{1,0:T(8,128)(2,1)}, u32[]{:S(2)}, u32[]{:S(2)}) %collective-permute-start.4) | collective-permute-done | bytes 786464 | tf_op jit(solution)/shard_map/ppermute | solution.py:117
  108.7 3.0 collective-permute-start.3
  111.7 1.1 collective-permute-start.13
  112.8 3.7 %constant_dynamic-slice_fusion.7 = bf16[512,3072]{1,0:T(8,128)(2,1)} fusion(bf16[512,6144]{1,0:T(8,128)(2,1)} %param.10, s32[]{:T(128)S(6)} %select_n.221), kind=kLoop, calls=%fused_computation.98 | loop fusion | bytes 6291460 | tf_op jit(solution)/shard_map/dynamic_slice | solution.py:120
  116.9 1.2 constant_dynamic-update-slice_fusion.11
  118.1 1.2 pad_maximum_fusion
  119.5 1.2 constant_dynamic-update-slice_fusion.9
  120.7 5.8 %collective-permute-done.3 = bf16[512,768]{1,0:T(8,128)(2,1)} collective-permute-done((bf16[512,768]{1,0:T(8,128)(2,1)}, bf16[512,768]{1,0:T(8,128)(2,1)}, u32[]{:S(2)}, u32[]{:S(2)}) %collective-permute-start.3) | collective-permute-done | bytes 786464 | tf_op jit(solution)/shard_map/ppermute | solution.py:117
  126.5 1.2 constant_dynamic-update-slice_fusion.8
  127.8 1.7 select_select_fusion
  129.4 10.2 %collective-permute-done.13 = bf16[768,768]{1,0:T(8,128)(2,1)} collective-permute-done((bf16[768,768]{1,0:T(8,128)(2,1)}, bf16[768,768]{1,0:T(8,128)(2,1)}, u32[]{:S(2)}, u32[]{:S(2)}) %collective-permute-start.13) | collective-permute-done | bytes 1179680 | tf_op jit(solution)/shard_map/ppermute | solution.py:117
  139.6 7.1 %fusion.11 = bf16[3072,768]{1,0:T(8,128)(2,1)} fusion(bf16[1024,768]{1,0:T(8,128)(2,1)S(1)} %pad_maximum_fusion, bf16[512,3072]{1,0:T(8,128)(2,1)S(1)} %constant_dynamic-update-slice_fusion.8, bf16[512,3072]{1,0:T(8,128)(2,1)S(1)} %copy-done.12), kind=kOutput, calls=%fused_computation.9 | convolution fusion | flops 4846780416 | bytes 12582912 | tf_op jit(solution)/shard_map/dot_general | solution.py:18
  146.8 2.1 constant_dynamic-slice_fusion.4
  149.9 17.5 %collective-permute-done.14 = bf16[512,768]{1,0:T(8,128)(2,1)} collective-permute-done((bf16[512,768]{1,0:T(8,128)(2,1)}, bf16[512,768]{1,0:T(8,128)(2,1)}, u32[]{:S(2)}, u32[]{:S(2)}) %collective-permute-start.14) | collective-permute-done | bytes 786464 | tf_op jit(solution)/shard_map/ppermute | solution.py:117
  167.5 2.6 collective-permute-start.15
  170.5 2.3 fusion.44
  172.8 2.3 fusion.40
  175.1 1.3 collective-permute-start.18
  176.4 1.9 fusion.34
  178.4 1.9 fusion.38
  180.3 2.3 fusion.42
  182.6 2.4 fusion.36
  185.0 2.1 fusion.46
  187.1 14.2 %collective-permute-done.18 = bf16[768,768]{1,0:T(8,128)(2,1)S(1)} collective-permute-done((bf16[768,768]{1,0:T(8,128)(2,1)S(1)}, bf16[768,768]{1,0:T(8,128)(2,1)S(1)}, u32[]{:S(2)}, u32[]{:S(2)}) %collective-permute-start.18) | collective-permute-done | bytes 1179680 | tf_op jit(solution)/shard_map/ppermute | solution.py:117
  201.3 2.3 add_convert_fusion.g
  203.6 2.4 value_grad.1
  206.0 1.3 collective-permute-start.19
  208.0 1.2 constant_dynamic-update-slice_fusion.7
  209.6 13.4 %collective-permute-done.19 = bf16[512,768]{1,0:T(8,128)(2,1)S(1)} collective-permute-done((bf16[512,768]{1,0:T(8,128)(2,1)S(1)}, bf16[512,768]{1,0:T(8,128)(2,1)S(1)}, u32[]{:S(2)}, u32[]{:S(2)}) %collective-permute-start.19) | collective-permute-done | bytes 786464 | tf_op jit(solution)/shard_map/ppermute | solution.py:117
  223.0 7.0 %fusion.8 = bf16[3072,768]{1,0:T(8,128)(2,1)} fusion(bf16[512,3072]{1,0:T(8,128)(2,1)S(1)} %constant_dynamic-update-slice_fusion.4, bf16[512,3072]{1,0:T(8,128)(2,1)S(1)} %constant_dynamic-slice_fusion.5, bf16[512,768]{1,0:T(8,128)(2,1)S(1)} %collective-permute-done.19, bf16[512,768]{1,0:T(8,128)(2,1)S(1)} %value_grad.1), kind=kOutput, calls=%fused_computation.8 | convolution fusion | flops 4849926144 | bytes 12582912 | tf_op jit(solution)/shard_map/dot_general | solution.py:18
  230.1 2.6 constant_dynamic-slice_fusion.3
  233.8 4.7 %collective-permute-start.20 = (bf16[512,128]{1,0:T(8,128)(2,1)S(1)}, bf16[512,128]{1,0:T(8,128)(2,1)}, u32[]{:S(2)}, u32[]{:S(2)}) collective-permute-start(bf16[512,128]{1,0:T(8,128)(2,1)S(1)} %get-tuple-element.56), channel_id=1, source_target_pairs={{0,8},{8,16},{16,24},{24,0},{1,9},{9,17},{17,25},{25,1},{2,10},{10... | collective-permute-start | bytes 393224 | tf_op jit(solution)/shard_map/ppermute | solution.py:117
  238.9 5.7 %fusion.31 = f32[128,768]{1,0:T(8,128)} fusion(bf16[512,768]{1,0:T(8,128)(2,1)S(1)} %value_grad.1, bf16[512,6144]{1,0:T(8,128)(2,1)} %param.9, bf16[1,6144,128]{2,1,0:T(8,128)(2,1)S(1)} %copy-done), kind=kOutput, calls=%fused_computation.31 | convolution fusion | flops 906035200 | bytes 9043968 | tf_op jit(solution)/shard_map/dot_general | solution.py:18
  246.5 2.0 collective-permute-start.30
  248.5 2.3 fusion.17
  251.2 3.3 collective-permute-start.24
  254.4 8.1 %score_grads.1 = (bf16[512,768]{1,0:T(8,128)(2,1)}, bf16[512,768]{1,0:T(8,128)(2,1)}) custom-call(bf16[512,768]{1,0:T(8,128)(2,1)S(1)} %copy-done.5, bf16[512,768]{1,0:T(8,128)(2,1)S(1)} %copy-done.7, bf16[512,768]{1,0:T(8,128)(2,1)S(1)} %copy-done.9, bf16[512,768]{1,0:T(8,128)(2,1)S(1)} %add_convert_fusion.g, s32[512,1]{1,0:T(8,128)S(1)} %copy.15.doc_col, ...), custom_call_target="tpu_custom_call" | custom-call | flops 1610612736 | bytes 5505024 | tf_op jit(solution)/shard_map/score_grads/pallas_call | solution.py:194
  263.8 10.0 %collective-permute-done.24 = bf16[384,128]{1,0:T(8,128)(2,1)S(1)} collective-permute-done((bf16[384,128]{1,0:T(8,128)(2,1)S(1)}, bf16[384,128]{1,0:T(8,128)(2,1)S(1)}, u32[]{:S(2)}, u32[]{:S(2)}) %collective-permute-start.24) | collective-permute-done | bytes 98336 | tf_op jit(solution)/shard_map/ppermute | solution.py:117
  273.9 2.1 collective-permute-start.26
  276.0 3.3 collective-permute-start.27
  279.4 1.6 fusion.58
  281.2 7.4 %collective-permute-done.27 = f32[384,128]{1,0:T(8,128)S(1)} collective-permute-done((f32[384,128]{1,0:T(8,128)S(1)}, f32[384,128]{1,0:T(8,128)S(1)}, u32[]{:S(2)}, u32[]{:S(2)}) %collective-permute-start.27) | collective-permute-done | bytes 196640 | tf_op jit(solution)/shard_map/ppermute | solution.py:117
  290.1 2.8 convert_multiply_fusion.1
  292.9 41.2 %reduce-scatter.5.cloned.1.call-done = bf16[768,768]{1,0:T(8,128)(2,1)} async-done(((bf16[3072,768]{1,0:T(8,128)(2,1)}), bf16[768,768]{1,0:T(8,128)(2,1)}) %reduce-scatter.5.cloned.1.call-update) | async-done | bytes 1179664 | tf_op jit(solution)/shard_map/reduce_scatter | solution.py:193
  334.1 2.8 convert_multiply_fusion
  (90 shorter events, 12.3 us)
Async XLA Ops:
  7.2 231.7 %copy-start = (bf16[1,6144,128]{2,1,0:T(8,128)(2,1)S(1)}, bf16[1,6144,128]{2,1,0:T(8,128)(2,1)}, u32[]{:S(2)}) copy-start(bf16[1,6144,128]{2,1,0:T(8,128)(2,1)} %param.16) | copy-start | bytes 4718596
  7.2 282.9 %reduce-scatter.3.cloned.1.call-start = ((), (), s32[]{:S(2)}) async-start(), calls=%async_computation.2 | async-start | bytes 5898240 | tf_op jit(solution)/shard_map/reduce_scatter | solution.py:182
  7.2 29.2 %collective-permute-start.6 = (bf16[768,768]{1,0:T(8,128)(2,1)}, bf16[768,768]{1,0:T(8,128)(2,1)S(1)}, u32[]{:S(2)}, u32[]{:S(2)}) collective-permute-start(bf16[768,768]{1,0:T(8,128)(2,1)} %param.15), channel_id=1, source_target_pairs={{1,0},{2,1},{3,2},{5,4},{6,5},{7,6},{9,8},{10,9},{11,10},{13,12},{... | collective-permute-start | bytes 3538952 | tf_op jit(solution)/shard_map/ppermute | solution.py:124
  9.3 29.0 %collective-permute-start.5 = (bf16[768,768]{1,0:T(8,128)(2,1)}, bf16[768,768]{1,0:T(8,128)(2,1)}, u32[]{:S(2)}, u32[]{:S(2)}) collective-permute-start(bf16[768,768]{1,0:T(8,128)(2,1)} %param.15), channel_id=1, source_target_pairs={{0,1},{1,2},{2,3},{4,5},{5,6},{6,7},{8,9},{9,10},{10,11},{12,13},{... | collective-permute-start | bytes 3538952 | tf_op jit(solution)/shard_map/ppermute | solution.py:124
  12.7 28.2 %collective-permute-start.7 = (bf16[768,768]{1,0:T(8,128)(2,1)}, bf16[768,768]{1,0:T(8,128)(2,1)}, u32[]{:S(2)}, u32[]{:S(2)}) collective-permute-start(bf16[768,768]{1,0:T(8,128)(2,1)} %param.15), channel_id=1, source_target_pairs={{0,4},{4,0},{1,5},{5,1},{2,6},{6,2},{3,7},{7,3},{8,12},{12,8},{9,1... | collective-permute-start | bytes 3538952 | tf_op jit(solution)/shard_map/ppermute | solution.py:117
  36.4 1.9 copy-start.10
  40.8 10.0 %copy-start.3 = (s32[512]{0:T(512)S(1)}, s32[512]{0:T(512)}, u32[]{:S(2)}) copy-start(s32[512]{0:T(512)} %param.14) | copy-start | bytes 6148
  40.8 10.1 %copy-start.4 = (bf16[512,768]{1,0:T(8,128)(2,1)S(1)}, bf16[512,768]{1,0:T(8,128)(2,1)}, u32[]{:S(2)}) copy-start(bf16[512,768]{1,0:T(8,128)(2,1)} %q.3) | copy-start | bytes 2359300
  40.8 32.7 %collective-permute-start.8 = (bf16[768,768]{1,0:T(8,128)(2,1)}, bf16[768,768]{1,0:T(8,128)(2,1)}, u32[]{:S(2)}, u32[]{:S(2)}) collective-permute-start(bf16[768,768]{1,0:T(8,128)(2,1)} %collective-permute-done.5), channel_id=1, source_target_pairs={{0,1},{1,2},{2,3},{4,5},{5,6},{6,7},{8,9},{9,10},{10,11},{12,13},{... | collective-permute-start | bytes 3538952 | tf_op jit(solution)/shard_map/ppermute | solution.py:124
  44.0 29.5 %collective-permute-start.9 = (bf16[768,768]{1,0:T(8,128)(2,1)}, bf16[768,768]{1,0:T(8,128)(2,1)}, u32[]{:S(2)}, u32[]{:S(2)}) collective-permute-start(bf16[768,768]{1,0:T(8,128)(2,1)} %copy-done.10), channel_id=1, source_target_pairs={{1,0},{2,1},{3,2},{5,4},{6,5},{7,6},{9,8},{10,9},{11,10},{13,12},{... | collective-permute-start | bytes 3538952 | tf_op jit(solution)/shard_map/ppermute | solution.py:124
  49.3 17.2 %collective-permute-start = (bf16[512,768]{1,0:T(8,128)(2,1)}, bf16[512,768]{1,0:T(8,128)(2,1)}, u32[]{:S(2)}, u32[]{:S(2)}) collective-permute-start(bf16[512,768]{1,0:T(8,128)(2,1)} %constant_dynamic-slice_fusion.6), channel_id=1, source_target_pairs={{0,4},{4,0},{1,5},{5,1},{2,6},{6,2},{3,7},{7,3},{8,12},{12,8},{9,1... | collective-permute-start | bytes 2359304 | tf_op jit(solution)/shard_map/ppermute | solution.py:117
  50.4 41.4 %collective-permute-start.10 = (bf16[768,768]{1,0:T(8,128)(2,1)}, bf16[768,768]{1,0:T(8,128)(2,1)}, u32[]{:S(2)}, u32[]{:S(2)}) collective-permute-start(bf16[768,768]{1,0:T(8,128)(2,1)} %broadcast_select_fusion), channel_id=1, source_target_pairs={{0,4},{4,0},{1,5},{5,1},{2,6},{6,2},{3,7},{7,3},{8,12},{12,8},{9,1... | collective-permute-start | bytes 3538952 | tf_op jit(solution)/shard_map/ppermute | solution.py:117
  50.9 1.1 copy-start.6
  52.1 1.1 copy-start.8
  53.2 20.3 %copy-start.11 = (bf16[768,768]{1,0:T(8,128)(2,1)S(1)}, bf16[768,768]{1,0:T(8,128)(2,1)}, u32[]{:S(2)}) copy-start(bf16[768,768]{1,0:T(8,128)(2,1)} %copy-done.10) | copy-start | bytes 3538948
  59.9 14.8 %copy-start.1 = (bf16[6,512,512]{2,1,0:T(8,128)(2,1)}, bf16[6,512,512]{2,1,0:T(8,128)(2,1)S(1)}, u32[]{:S(2)}) copy-start(bf16[6,512,512]{2,1,0:T(8,128)(2,1)S(1)} %get-tuple-element.34.half) | copy-start | bytes 9437188
  60.0 48.7 %collective-permute-start.4 = (bf16[512,768]{1,0:T(8,128)(2,1)S(1)}, bf16[512,768]{1,0:T(8,128)(2,1)}, u32[]{:S(2)}, u32[]{:S(2)}) collective-permute-start(bf16[512,768]{1,0:T(8,128)(2,1)S(1)} %get-tuple-element.25), channel_id=1, source_target_pairs={{0,4},{4,0},{1,5},{5,1},{2,6},{6,2},{3,7},{7,3},{8,12},{12,8},{9,1... | collective-permute-start | bytes 2359304 | tf_op jit(solution)/shard_map/ppermute | solution.py:117
  66.6 45.2 %collective-permute-start.1 = (bf16[512,768]{1,0:T(8,128)(2,1)}, bf16[512,768]{1,0:T(8,128)(2,1)S(1)}, u32[]{:S(2)}, u32[]{:S(2)}) collective-permute-start(bf16[512,768]{1,0:T(8,128)(2,1)} %collective-permute-done), channel_id=1, source_target_pairs={{0,8},{8,16},{16,24},{24,0},{1,9},{9,17},{17,25},{25,1},{2,10},{10... | collective-permute-start | bytes 2359304 | tf_op jit(solution)/shard_map/ppermute | solution.py:117
  91.8 35.9 %collective-permute-start.11 = (bf16[768,768]{1,0:T(8,128)(2,1)}, bf16[768,768]{1,0:T(8,128)(2,1)}, u32[]{:S(2)}, u32[]{:S(2)}) collective-permute-start(bf16[768,768]{1,0:T(8,128)(2,1)} %collective-permute-done.8), channel_id=1, source_target_pairs={{0,1},{1,2},{2,3},{4,5},{5,6},{6,7},{8,9},{9,10},{10,11},{12,13},{... | collective-permute-start | bytes 3538952 | tf_op jit(solution)/shard_map/ppermute | solution.py:124
  93.8 34.0 %collective-permute-start.12 = (bf16[768,768]{1,0:T(8,128)(2,1)}, bf16[768,768]{1,0:T(8,128)(2,1)}, u32[]{:S(2)}, u32[]{:S(2)}) collective-permute-start(bf16[768,768]{1,0:T(8,128)(2,1)} %collective-permute-done.9), channel_id=1, source_target_pairs={{1,0},{2,1},{3,2},{5,4},{6,5},{7,6},{9,8},{10,9},{11,10},{13,12},{... | collective-permute-start | bytes 3538952 | tf_op jit(solution)/shard_map/ppermute | solution.py:124
  98.1 21.4 %collective-permute-start.2 = (bf16[512,768]{1,0:T(8,128)(2,1)}, bf16[512,768]{1,0:T(8,128)(2,1)}, u32[]{:S(2)}, u32[]{:S(2)}) collective-permute-start(bf16[512,768]{1,0:T(8,128)(2,1)} %collective-permute-done), channel_id=1, source_target_pairs={{0,16},{8,24},{16,0},{24,8},{1,17},{9,25},{17,1},{25,9},{2,18},{10... | collective-permute-start | bytes 2359304 | tf_op jit(solution)/shard_map/ppermute | solution.py:117
  108.7 17.8 %collective-permute-start.3 = (bf16[512,768]{1,0:T(8,128)(2,1)}, bf16[512,768]{1,0:T(8,128)(2,1)}, u32[]{:S(2)}, u32[]{:S(2)}) collective-permute-start(bf16[512,768]{1,0:T(8,128)(2,1)} %collective-permute-done), channel_id=1, source_target_pairs={{0,24},{8,0},{16,8},{24,16},{1,25},{9,1},{17,9},{25,17},{2,26},{10... | collective-permute-start | bytes 2359304 | tf_op jit(solution)/shard_map/ppermute | solution.py:117
  111.7 27.9 %collective-permute-start.13 = (bf16[768,768]{1,0:T(8,128)(2,1)}, bf16[768,768]{1,0:T(8,128)(2,1)}, u32[]{:S(2)}, u32[]{:S(2)}) collective-permute-start(bf16[768,768]{1,0:T(8,128)(2,1)} %select_select_fusion.1), channel_id=1, source_target_pairs={{0,4},{4,0},{1,5},{5,1},{2,6},{6,2},{3,7},{7,3},{8,12},{12,8},{9,1... | collective-permute-start | bytes 3538952 | tf_op jit(solution)/shard_map/ppermute | solution.py:117
  127.7 11.9 %copy-start.12 = (bf16[512,3072]{1,0:T(8,128)(2,1)S(1)}, bf16[512,3072]{1,0:T(8,128)(2,1)}, u32[]{:S(2)}) copy-start(bf16[512,3072]{1,0:T(8,128)(2,1)} %constant_dynamic-slice_fusion.7) | copy-start | bytes 9437188
  146.7 187.4 %reduce-scatter.5.cloned.1.call-start = ((), (), s32[]{:S(2)}) async-start(), calls=%async_computation.3 | async-start | bytes 5898240 | tf_op jit(solution)/shard_map/reduce_scatter | solution.py:193
  148.9 18.6 %collective-permute-start.14 = (bf16[512,768]{1,0:T(8,128)(2,1)}, bf16[512,768]{1,0:T(8,128)(2,1)}, u32[]{:S(2)}, u32[]{:S(2)}) collective-permute-start(bf16[512,768]{1,0:T(8,128)(2,1)} %constant_dynamic-slice_fusion.4), channel_id=1, source_target_pairs={{0,4},{4,0},{1,5},{5,1},{2,6},{6,2},{3,7},{7,3},{8,12},{12,8},{9,1... | collective-permute-start | bytes 2359304 | tf_op jit(solution)/shard_map/ppermute | solution.py:117
  167.5 41.8 %collective-permute-start.15 = (bf16[512,768]{1,0:T(8,128)(2,1)}, bf16[512,768]{1,0:T(8,128)(2,1)S(1)}, u32[]{:S(2)}, u32[]{:S(2)}) collective-permute-start(bf16[512,768]{1,0:T(8,128)(2,1)} %collective-permute-done.14), channel_id=1, source_target_pairs={{0,8},{8,16},{16,24},{24,0},{1,9},{9,17},{17,25},{25,1},{2,10},{10... | collective-permute-start | bytes 2359304 | tf_op jit(solution)/shard_map/ppermute | solution.py:117
  170.1 39.3 %collective-permute-start.16 = (bf16[512,768]{1,0:T(8,128)(2,1)}, bf16[512,768]{1,0:T(8,128)(2,1)S(1)}, u32[]{:S(2)}, u32[]{:S(2)}) collective-permute-start(bf16[512,768]{1,0:T(8,128)(2,1)} %collective-permute-done.14), channel_id=1, source_target_pairs={{0,16},{8,24},{16,0},{24,8},{1,17},{9,25},{17,1},{25,9},{2,18},{10... | collective-permute-start | bytes 2359304 | tf_op jit(solution)/shard_map/ppermute | solution.py:117
  170.5 39.0 %collective-permute-start.17 = (bf16[512,768]{1,0:T(8,128)(2,1)}, bf16[512,768]{1,0:T(8,128)(2,1)S(1)}, u32[]{:S(2)}, u32[]{:S(2)}) collective-permute-start(bf16[512,768]{1,0:T(8,128)(2,1)} %collective-permute-done.14), channel_id=1, source_target_pairs={{0,24},{8,0},{16,8},{24,16},{1,25},{9,1},{17,9},{25,17},{2,26},{10... | collective-permute-start | bytes 2359304 | tf_op jit(solution)/shard_map/ppermute | solution.py:117
  175.1 3.3 copy-start.13
  175.1 26.2 %collective-permute-start.18 = (bf16[768,768]{1,0:T(8,128)(2,1)S(1)}, bf16[768,768]{1,0:T(8,128)(2,1)S(1)}, u32[]{:S(2)}, u32[]{:S(2)}) collective-permute-start(bf16[768,768]{1,0:T(8,128)(2,1)S(1)} %select_select_fusion), channel_id=1, source_target_pairs={{0,4},{4,0},{1,5},{5,1},{2,6},{6,2},{3,7},{7,3},{8,12},{12,8},{9,1... | collective-permute-start | bytes 3538952 | tf_op jit(solution)/shard_map/ppermute | solution.py:117
  182.6 2.4 copy-start.15
  185.0 22.3 %slice-start = ((s8[6291456]{0:T(1024)(128)(4,1)}), s8[4194304]{0:T(1024)(128)(4,1)S(1)}, s32[]{:S(2)}) async-start(s8[6291456]{0:T(1024)(128)(4,1)} %bitcast.64), calls=%async_computation.4 | async-start | bytes 8388608
  187.1 20.3 %slice-start.1 = ((s8[6291456]{0:T(1024)(128)(4,1)}), s8[2097152]{0:T(1024)(128)(4,1)S(1)}, s32[]{:S(2)}) async-start(s8[6291456]{0:T(1024)(128)(4,1)} %bitcast.64), calls=%async_computation.5 | async-start | bytes 4194304
  201.3 2.3 copy-start.2
  206.0 16.9 %collective-permute-start.19 = (bf16[512,768]{1,0:T(8,128)(2,1)S(1)}, bf16[512,768]{1,0:T(8,128)(2,1)S(1)}, u32[]{:S(2)}, u32[]{:S(2)}) collective-permute-start(bf16[512,768]{1,0:T(8,128)(2,1)S(1)} %value_grad.1), channel_id=1, source_target_pairs={{0,4},{4,0},{1,5},{5,1},{2,6},{6,2},{3,7},{7,3},{8,12},{12,8},{9,1... | collective-permute-start | bytes 2359304 | tf_op jit(solution)/shard_map/ppermute | solution.py:117
  230.1 2.6 copy-start.14
  233.8 14.7 %collective-permute-start.20 = (bf16[512,128]{1,0:T(8,128)(2,1)S(1)}, bf16[512,128]{1,0:T(8,128)(2,1)}, u32[]{:S(2)}, u32[]{:S(2)}) collective-permute-start(bf16[512,128]{1,0:T(8,128)(2,1)S(1)} %get-tuple-element.56), channel_id=1, source_target_pairs={{0,8},{8,16},{16,24},{24,0},{1,9},{9,17},{17,25},{25,1},{2,10},{10... | collective-permute-start | bytes 393224 | tf_op jit(solution)/shard_map/ppermute | solution.py:117
  238.4 10.1 %collective-permute-start.21 = (bf16[512,128]{1,0:T(8,128)(2,1)S(1)}, bf16[512,128]{1,0:T(8,128)(2,1)}, u32[]{:S(2)}, u32[]{:S(2)}) collective-permute-start(bf16[512,128]{1,0:T(8,128)(2,1)S(1)} %get-tuple-element.56), channel_id=1, source_target_pairs={{0,16},{8,24},{16,0},{24,8},{1,17},{9,25},{17,1},{25,9},{2,18},{10... | collective-permute-start | bytes 393224 | tf_op jit(solution)/shard_map/ppermute | solution.py:117
  238.4 10.1 %collective-permute-start.22 = (bf16[512,128]{1,0:T(8,128)(2,1)S(1)}, bf16[512,128]{1,0:T(8,128)(2,1)}, u32[]{:S(2)}, u32[]{:S(2)}) collective-permute-start(bf16[512,128]{1,0:T(8,128)(2,1)S(1)} %get-tuple-element.56), channel_id=1, source_target_pairs={{0,24},{8,0},{16,8},{24,16},{1,25},{9,1},{17,9},{25,17},{2,26},{10... | collective-permute-start | bytes 393224 | tf_op jit(solution)/shard_map/ppermute | solution.py:117
  245.6 33.8 %collective-permute-start.29 = (bf16[32,768]{1,0:T(8,128)(2,1)S(1)}, bf16[32,768]{1,0:T(8,128)(2,1)S(1)}, u32[]{:S(2)}, u32[]{:S(2)}) collective-permute-start(bf16[32,768]{1,0:T(8,128)(2,1)S(1)} %get-tuple-element.53), channel_id=1, source_target_pairs={{0,1},{1,2},{2,3},{3,0},{4,5},{5,6},{6,7},{7,4},{8,9},{9,10},{10,1... | collective-permute-start | bytes 147464 | tf_op jit(solution)/shard_map/ppermute | solution.py:117
  246.5 32.9 %collective-permute-start.30 = (bf16[32,768]{1,0:T(8,128)(2,1)S(1)}, bf16[32,768]{1,0:T(8,128)(2,1)S(1)}, u32[]{:S(2)}, u32[]{:S(2)}) collective-permute-start(bf16[32,768]{1,0:T(8,128)(2,1)S(1)} %get-tuple-element.55), channel_id=1, source_target_pairs={{0,2},{1,3},{2,0},{3,1},{4,6},{5,7},{6,4},{7,5},{8,10},{9,11},{10,... | collective-permute-start | bytes 147464 | tf_op jit(solution)/shard_map/ppermute | solution.py:117
  248.5 5.9 %copy-start.5 = (bf16[512,768]{1,0:T(8,128)(2,1)S(1)}, bf16[512,768]{1,0:T(8,128)(2,1)}, u32[]{:S(2)}) copy-start(bf16[512,768]{1,0:T(8,128)(2,1)} %q.3) | copy-start | bytes 2359300
  248.5 5.9 %copy-start.7 = (bf16[512,768]{1,0:T(8,128)(2,1)S(1)}, bf16[512,768]{1,0:T(8,128)(2,1)}, u32[]{:S(2)}) copy-start(bf16[512,768]{1,0:T(8,128)(2,1)} %k.3) | copy-start | bytes 2359300
  248.5 5.9 %copy-start.9 = (bf16[512,768]{1,0:T(8,128)(2,1)S(1)}, bf16[512,768]{1,0:T(8,128)(2,1)}, u32[]{:S(2)}) copy-start(bf16[512,768]{1,0:T(8,128)(2,1)} %v.3) | copy-start | bytes 2359300
  250.9 12.2 %collective-permute-start.23 = (bf16[384,128]{1,0:T(8,128)(2,1)S(1)}, bf16[384,128]{1,0:T(8,128)(2,1)S(1)}, u32[]{:S(2)}, u32[]{:S(2)}) collective-permute-start(bf16[384,128]{1,0:T(8,128)(2,1)S(1)} %get-tuple-element.50), channel_id=1, source_target_pairs={{0,1},{1,2},{2,3},{3,0},{4,5},{5,6},{6,7},{7,4},{8,9},{9,10},{10,1... | collective-permute-start | bytes 294920 | tf_op jit(solution)/shard_map/ppermute | solution.py:117
  251.2 22.6 %collective-permute-start.24 = (bf16[384,128]{1,0:T(8,128)(2,1)S(1)}, bf16[384,128]{1,0:T(8,128)(2,1)S(1)}, u32[]{:S(2)}, u32[]{:S(2)}) collective-permute-start(bf16[384,128]{1,0:T(8,128)(2,1)S(1)} %get-tuple-element.52), channel_id=1, source_target_pairs={{0,2},{1,3},{2,0},{3,1},{4,6},{5,7},{6,4},{7,5},{8,10},{9,11},{10,... | collective-permute-start | bytes 294920 | tf_op jit(solution)/shard_map/ppermute | solution.py:117
  254.4 19.4 %collective-permute-start.25 = (bf16[384,128]{1,0:T(8,128)(2,1)S(1)}, bf16[384,128]{1,0:T(8,128)(2,1)S(1)}, u32[]{:S(2)}, u32[]{:S(2)}) collective-permute-start(bf16[384,128]{1,0:T(8,128)(2,1)S(1)} %get-tuple-element.51), channel_id=1, source_target_pairs={{0,3},{1,0},{2,1},{3,2},{4,7},{5,4},{6,5},{7,6},{8,11},{9,8},{10,9... | collective-permute-start | bytes 294920 | tf_op jit(solution)/shard_map/ppermute | solution.py:117
  263.1 16.3 %collective-permute-start.31 = (bf16[32,768]{1,0:T(8,128)(2,1)S(1)}, bf16[32,768]{1,0:T(8,128)(2,1)S(1)}, u32[]{:S(2)}, u32[]{:S(2)}) collective-permute-start(bf16[32,768]{1,0:T(8,128)(2,1)S(1)} %get-tuple-element.54), channel_id=1, source_target_pairs={{0,3},{1,0},{2,1},{3,2},{4,7},{5,4},{6,5},{7,6},{8,11},{9,8},{10,9... | collective-permute-start | bytes 147464 | tf_op jit(solution)/shard_map/ppermute | solution.py:117
  273.9 7.2 %collective-permute-start.26 = (f32[384,128]{1,0:T(8,128)S(1)}, f32[384,128]{1,0:T(8,128)S(1)}, u32[]{:S(2)}, u32[]{:S(2)}) collective-permute-start(f32[384,128]{1,0:T(8,128)S(1)} %get-tuple-element.45), channel_id=1, source_target_pairs={{0,8},{8,16},{16,24},{24,0},{1,9},{9,17},{17,25},{25,1},{2,10},{10... | collective-permute-start | bytes 589832 | tf_op jit(solution)/shard_map/ppermute | solution.py:117
  276.0 12.5 %collective-permute-start.27 = (f32[384,128]{1,0:T(8,128)S(1)}, f32[384,128]{1,0:T(8,128)S(1)}, u32[]{:S(2)}, u32[]{:S(2)}) collective-permute-start(f32[384,128]{1,0:T(8,128)S(1)} %get-tuple-element.45), channel_id=1, source_target_pairs={{0,16},{8,24},{16,0},{24,8},{1,17},{9,25},{17,1},{25,9},{2,18},{10... | collective-permute-start | bytes 589832 | tf_op jit(solution)/shard_map/ppermute | solution.py:117
  280.9 8.2 %collective-permute-start.28 = (f32[384,128]{1,0:T(8,128)S(1)}, f32[384,128]{1,0:T(8,128)S(1)}, u32[]{:S(2)}, u32[]{:S(2)}) collective-permute-start(f32[384,128]{1,0:T(8,128)S(1)} %get-tuple-element.45), channel_id=1, source_target_pairs={{0,24},{8,0},{16,8},{24,16},{1,25},{9,1},{17,9},{25,17},{2,26},{10... | collective-permute-start | bytes 589832 | tf_op jit(solution)/shard_map/ppermute | solution.py:117
Sparse Core Ops, SparseCore 0:
  146.9 86.4 reduce-scatter.2
  235.7 98.4 reduce-scatter.4

commit v4 on v3

--- a/solution.py
+++ b/solution.py
@@ -155,18 +155,18 @@
         hops = {hop: jnp.int32(hop) for hop in arrivals}
         slots.append((dp - pick(choices, hops), here, forwards(here)))
 
-    def regroup(x):
+    def regroup(x, beside):
         gathered = [columns(x, sec * part, part)]
         for j in range(1, n_sec):
             sent = columns(x, ((sec + j) % n_sec) * part + ten * piece, piece)
-            mine = shift(sent, "section", j)
+            mine, beside = lax.optimization_barrier((shift(sent, "section", j), beside))
             whole = jnp.zeros((rows, part), x.dtype)
             for m in range(n_ten):
                 got = mine if m == 0 else shift(mine, "tensor", m)
                 place = ((ten + n_ten - m) % n_ten) * piece
                 whole = lax.dynamic_update_slice_in_dim(whole, got, place, 1)
             gathered.append(whole)
-        return jnp.concatenate(gathered, axis=0)
+        return jnp.concatenate(gathered, axis=0), beside
 
     def across_sections(x):
         return jnp.concatenate([x] + [shift(x, "section", j) for j in range(1, n_sec)], axis=0)
@@ -174,13 +174,15 @@
     forward, value, scores = attention_calls(rows, local_width)
     doc_col, doc_row = document_index[:, None], document_index[None, :]
     output, probs_half = forward(queries, saved_keys, values, doc_col, doc_row)
-    grad_rows = regroup(output_gradient)
+    grad_rows, _ = regroup(output_gradient, [])
     output_rows, kept = lax.optimization_barrier(
         (across_sections(output), [here for _, here, _ in slots])
     )
     out_term = dot(grad_rows, output_rows, TN).astype(BF16)
     out_sum = lax.psum_scatter(out_term, "dp", scatter_dimension=0, tiled=True)
 
+    input_rows, last = regroup(block_input, slots[-1][2])
+    slots[-1] = (*slots[-1][:2], last)
     attn_grad = jnp.zeros((rows, local_width), F32)
     for (owner_dp, _, sent), here in zip(slots, kept):
         for j, shard in enumerate([here] + list(sent)):
@@ -189,7 +191,7 @@
     attn_grad = attn_grad.astype(BF16)
 
     value_gradient = value(probs_half, attn_grad)
-    value_term = dot(regroup(block_input), across_sections(value_gradient), TN).astype(BF16)
+    value_term = dot(input_rows, across_sections(value_gradient), TN).astype(BF16)
     value_sum = lax.psum_scatter(value_term, "dp", scatter_dimension=0, tiled=True)
     grad_query, grad_key = scores(
         queries, saved_keys, values, attn_grad, doc_col, doc_row

time: 345 us -> 348 us (level)
  waiting for transfers between devices: 178 us -> 187 us
  starting transfers between devices: 58.5 us -> 50.7 us
    ppermute x26, waiting for transfers between devices: 112 us -> 122 us  [shift(): return lax.ppermute(x, axis, [(i, (i + by) % size) for i in range(size)])]
    ppermute x26, starting transfers between devices: 40.3 us -> 32.6 us  [shift(): return lax.ppermute(x, axis, [(i, (i + by) % size) for i in range(size)])]
  transfers between devices with their start and end apart: 34 -> 34, of which waited for: 15 -> 19; matrix products, arithmetic and copies ran while one was open for 19% -> 19% of each run, Pallas kernels for 5% -> 5%
where the time goes in v4:
time: 348 us; the launch traced here: 346 us
  waiting for transfers between devices  187 us (54%)
  starting transfers between devices  50.7 us (15%)
  matrix products  41.9 us (12%)
  local copies, waits for them, and re-layouts  20.4 us (6%)
  Pallas kernels  17.3 us (5%)
  other arithmetic  14.8 us (4%)
  between operations  14.6 us (4%)
    ppermute x26, waiting for transfers between devices, shift(): return lax.ppermute(x, axis, [(i, (i + by) % size) for i in range(size)])  122 us
    dot_general x13, matrix products, dot(): return lax.dot_general(a, b, dims, preferred_element_type=F32)  41.9 us
    reduce_scatter x1, waiting for transfers between devices, local(): lax.psum_scatter(value_term, 'dp', scatter_dimension=0, tiled=True)  40.4 us
    ppermute x26, starting transfers between devices, shift(): return lax.ppermute(x, axis, [(i, (i + by) % size) for i in range(size)])  32.6 us
    ppermute x6, waiting for transfers between devices, step(): return lax.ppermute(x, 'dp', pairs)  24.4 us
    ppermute x6, starting transfers between devices, step(): return lax.ppermute(x, 'dp', pairs)  18.1 us
    dynamic_slice x5, local copies, waits for them, and re-layouts, columns(): return lax.dynamic_slice_in_dim(x, start, size, 1)  10.7 us
    pallas_call x1, Pallas kernels, local(): scores(queries, saved_keys, values, attn_grad, doc_col, doc_row)  8.15 us
  transfers between devices with their start and end apart: 34, of which 19 were waited for; matrix products, arithmetic and copies ran while one was open for 19% of the time, Pallas kernels for 5%

profile of v4, /device:TPU:9, one launch (start us, length us, event | category | flops | bytes accessed | tf_op | source)
XLA Modules:
  0.0 346.4 jit_solution(4682586549320306216)
XLA Ops:
  7.2 2.1 collective-permute-start.6
  9.3 3.4 collective-permute-start.5
  12.7 1.3 collective-permute-start.7
  14.0 22.4 %collective-permute-done.6 = bf16[768,768]{1,0:T(8,128)(2,1)S(1)} collective-permute-done((bf16[768,768]{1,0:T(8,128)(2,1)}, bf16[768,768]{1,0:T(8,128)(2,1)S(1)}, u32[]{:S(2)}, u32[]{:S(2)}) %collective-permute-start.6) | collective-permute-done | bytes 1179680 | tf_op jit(solution)/shard_map/ppermute | solution.py:124
  36.4 1.9 collective-permute-done.5
  38.3 2.5 broadcast_select_fusion
  40.8 3.2 collective-permute-start.8
  44.0 3.2 collective-permute-start.9
  47.2 2.1 constant_dynamic-slice_fusion.6
  51.0 1.1 copy-done.6
  52.1 1.1 copy-done.8
  53.2 6.7 %attend_out.1 = (bf16[512,768]{1,0:T(8,128)(2,1)S(1)}, bf16[6,512,512]{2,1,0:T(8,128)(2,1)S(1)}) custom-call(bf16[512,768]{1,0:T(8,128)(2,1)S(1)} %copy-done.4, bf16[512,768]{1,0:T(8,128)(2,1)S(1)} %copy-done.6, bf16[512,768]{1,0:T(8,128)(2,1)S(1)} %copy-done.8, s32[512,1]{1,0:T(8,128)S(1)} %copy.15.doc_col, s32[1,512]{1,0:T(1,128)S(1)} %bitcast.62), custom_call_target="tpu_custom_call" | custom-call | flops 805306368 | bytes 4718592 | tf_op jit(solution)/shard_map/attend_out/pallas_call | solution.py:176
  60.0 1.1 collective-permute-start.4
  61.1 5.5 %collective-permute-done = bf16[512,768]{1,0:T(8,128)(2,1)} collective-permute-done((bf16[512,768]{1,0:T(8,128)(2,1)}, bf16[512,768]{1,0:T(8,128)(2,1)}, u32[]{:S(2)}, u32[]{:S(2)}) %collective-permute-start) | collective-permute-done | bytes 786464 | tf_op jit(solution)/shard_map/ppermute | solution.py:117
  66.6 6.9 %collective-permute-start.1 = (bf16[512,768]{1,0:T(8,128)(2,1)}, bf16[512,768]{1,0:T(8,128)(2,1)S(1)}, u32[]{:S(2)}, u32[]{:S(2)}) collective-permute-start(bf16[512,768]{1,0:T(8,128)(2,1)} %collective-permute-done), channel_id=1, source_target_pairs={{0,8},{8,16},{16,24},{24,0},{1,9},{9,17},{17,25},{25,1},{2,10},{10... | collective-permute-start | bytes 2359304 | tf_op jit(solution)/shard_map/ppermute | solution.py:117
  73.5 1.2 select_select_fusion.1
  74.7 17.1 %collective-permute-done.10 = bf16[768,768]{1,0:T(8,128)(2,1)} collective-permute-done((bf16[768,768]{1,0:T(8,128)(2,1)}, bf16[768,768]{1,0:T(8,128)(2,1)}, u32[]{:S(2)}, u32[]{:S(2)}) %collective-permute-start.10) | collective-permute-done | bytes 1179680 | tf_op jit(solution)/shard_map/ppermute | solution.py:117
  91.8 1.9 collective-permute-start.11
  93.8 4.4 %collective-permute-start.12 = (bf16[768,768]{1,0:T(8,128)(2,1)}, bf16[768,768]{1,0:T(8,128)(2,1)}, u32[]{:S(2)}, u32[]{:S(2)}) collective-permute-start(bf16[768,768]{1,0:T(8,128)(2,1)} %collective-permute-done.9), channel_id=1, source_target_pairs={{1,0},{2,1},{3,2},{5,4},{6,5},{7,6},{9,8},{10,9},{11,10},{13,12},{... | collective-permute-start | bytes 3538952 | tf_op jit(solution)/shard_map/ppermute | solution.py:124
  98.9 9.8 %collective-permute-done.4 = bf16[512,768]{1,0:T(8,128)(2,1)} collective-permute-done((bf16[512,768]{1,0:T(8,128)(2,1)S(1)}, bf16[512,768]{1,0:T(8,128)(2,1)}, u32[]{:S(2)}, u32[]{:S(2)}) %collective-permute-start.4) | collective-permute-done | bytes 786464 | tf_op jit(solution)/shard_map/ppermute | solution.py:117
  108.7 3.0 collective-permute-start.3
  112.8 3.7 %constant_dynamic-slice_fusion.7 = bf16[512,3072]{1,0:T(8,128)(2,1)} fusion(bf16[512,6144]{1,0:T(8,128)(2,1)} %param.10, s32[]{:T(128)S(6)} %select_n.221), kind=kLoop, calls=%fused_computation.98 | loop fusion | bytes 6291460 | tf_op jit(solution)/shard_map/dynamic_slice | solution.py:120
  116.9 1.2 constant_dynamic-update-slice_fusion.11
  118.1 1.2 pad_maximum_fusion
  119.5 1.2 constant_dynamic-update-slice_fusion.9
  120.7 5.8 %collective-permute-done.3 = bf16[512,768]{1,0:T(8,128)(2,1)} collective-permute-done((bf16[512,768]{1,0:T(8,128)(2,1)}, bf16[512,768]{1,0:T(8,128)(2,1)}, u32[]{:S(2)}, u32[]{:S(2)}) %collective-permute-start.3) | collective-permute-done | bytes 786464 | tf_op jit(solution)/shard_map/ppermute | solution.py:117
  126.5 1.2 constant_dynamic-update-slice_fusion.8
  127.8 1.7 select_select_fusion
  129.4 10.2 %collective-permute-done.13 = bf16[768,768]{1,0:T(8,128)(2,1)} collective-permute-done((bf16[768,768]{1,0:T(8,128)(2,1)}, bf16[768,768]{1,0:T(8,128)(2,1)}, u32[]{:S(2)}, u32[]{:S(2)}) %collective-permute-start.13) | collective-permute-done | bytes 1179680 | tf_op jit(solution)/shard_map/ppermute | solution.py:117
  139.6 7.1 %fusion.11 = bf16[3072,768]{1,0:T(8,128)(2,1)} fusion(bf16[1024,768]{1,0:T(8,128)(2,1)S(1)} %pad_maximum_fusion, bf16[512,3072]{1,0:T(8,128)(2,1)S(1)} %constant_dynamic-update-slice_fusion.8, bf16[512,3072]{1,0:T(8,128)(2,1)S(1)} %copy-done.12), kind=kOutput, calls=%fused_computation.9 | convolution fusion | flops 4846780416 | bytes 12582912 | tf_op jit(solution)/shard_map/dot_general | solution.py:18
  146.8 2.1 constant_dynamic-slice_fusion.4
  149.9 2.3 fusion.44
  152.2 2.3 fusion.40
  155.0 2.2 fusion.34
  157.3 1.9 fusion.38
  159.2 2.3 fusion.42
  161.5 2.4 fusion.36
  163.9 2.1 fusion.46
  166.0 1.4 collective-permute-done.14
  167.5 25.3 %collective-permute-done.15 = bf16[768,768]{1,0:T(8,128)(2,1)S(1)} collective-permute-done((bf16[768,768]{1,0:T(8,128)(2,1)S(1)}, bf16[768,768]{1,0:T(8,128)(2,1)S(1)}, u32[]{:S(2)}, u32[]{:S(2)}) %collective-permute-start.15) | collective-permute-done | bytes 1179680 | tf_op jit(solution)/shard_map/ppermute | solution.py:117
  192.7 2.5 collective-permute-start.16
  195.7 2.3 add_convert_fusion.g
  198.0 2.4 value_grad.1
  200.4 1.3 collective-permute-start.19
  202.4 1.2 constant_dynamic-update-slice_fusion.7
  203.6 8.8 %collective-permute-done.16 = bf16[512,768]{1,0:T(8,128)(2,1)S(1)} collective-permute-done((bf16[512,768]{1,0:T(8,128)(2,1)}, bf16[512,768]{1,0:T(8,128)(2,1)S(1)}, u32[]{:S(2)}, u32[]{:S(2)}) %collective-permute-start.16) | collective-permute-done | bytes 786464 | tf_op jit(solution)/shard_map/ppermute | solution.py:117
  212.5 17.9 %collective-permute-done.17 = bf16[512,768]{1,0:T(8,128)(2,1)S(1)} collective-permute-done((bf16[512,768]{1,0:T(8,128)(2,1)}, bf16[512,768]{1,0:T(8,128)(2,1)S(1)}, u32[]{:S(2)}, u32[]{:S(2)}) %collective-permute-start.17) | collective-permute-done | bytes 786464 | tf_op jit(solution)/shard_map/ppermute | solution.py:117
  231.0 7.0 %fusion.8 = bf16[3072,768]{1,0:T(8,128)(2,1)} fusion(bf16[512,3072]{1,0:T(8,128)(2,1)S(1)} %constant_dynamic-update-slice_fusion.4, bf16[512,3072]{1,0:T(8,128)(2,1)S(1)} %constant_dynamic-slice_fusion.5, bf16[512,768]{1,0:T(8,128)(2,1)S(1)} %collective-permute-done.19, bf16[512,768]{1,0:T(8,128)(2,1)S(1)} %value_grad.1), kind=kOutput, calls=%fused_computation.8 | convolution fusion | flops 4849926144 | bytes 12582912 | tf_op jit(solution)/shard_map/dot_general | solution.py:18
  238.2 2.6 constant_dynamic-slice_fusion.3
  243.7 6.6 %fusion.31 = f32[128,768]{1,0:T(8,128)} fusion(bf16[512,768]{1,0:T(8,128)(2,1)S(1)} %value_grad.1, bf16[512,6144]{1,0:T(8,128)(2,1)} %param.9, bf16[1,6144,128]{2,1,0:T(8,128)(2,1)S(1)} %copy-done), kind=kOutput, calls=%fused_computation.31 | convolution fusion | flops 906035200 | bytes 9043968 | tf_op jit(solution)/shard_map/dot_general | solution.py:18
  251.3 2.4 collective-permute-start.30
  253.8 2.4 fusion.17
  256.4 3.3 collective-permute-start.24
  259.7 8.1 %score_grads.1 = (bf16[512,768]{1,0:T(8,128)(2,1)}, bf16[512,768]{1,0:T(8,128)(2,1)}) custom-call(bf16[512,768]{1,0:T(8,128)(2,1)S(1)} %copy-done.5, bf16[512,768]{1,0:T(8,128)(2,1)S(1)} %copy-done.7, bf16[512,768]{1,0:T(8,128)(2,1)S(1)} %copy-done.9, bf16[512,768]{1,0:T(8,128)(2,1)S(1)} %add_convert_fusion.g, s32[512,1]{1,0:T(8,128)S(1)} %copy.15.doc_col, ...), custom_call_target="tpu_custom_call" | custom-call | flops 1610612736 | bytes 5505024 | tf_op jit(solution)/shard_map/score_grads/pallas_call | solution.py:196
  267.9 1.2 collective-permute-start.31
  269.0 7.8 %collective-permute-done.24 = bf16[384,128]{1,0:T(8,128)(2,1)S(1)} collective-permute-done((bf16[384,128]{1,0:T(8,128)(2,1)S(1)}, bf16[384,128]{1,0:T(8,128)(2,1)S(1)}, u32[]{:S(2)}, u32[]{:S(2)}) %collective-permute-start.24) | collective-permute-done | bytes 98336 | tf_op jit(solution)/shard_map/ppermute | solution.py:117
  276.9 4.0 %collective-permute-done.25 = bf16[384,128]{1,0:T(8,128)(2,1)S(1)} collective-permute-done((bf16[384,128]{1,0:T(8,128)(2,1)S(1)}, bf16[384,128]{1,0:T(8,128)(2,1)S(1)}, u32[]{:S(2)}, u32[]{:S(2)}) %collective-permute-start.25) | collective-permute-done | bytes 98336 | tf_op jit(solution)/shard_map/ppermute | solution.py:117
  280.9 1.3 collective-permute-start.26
  283.1 1.6 fusion.58
  285.0 1.4 collective-permute-done.26
  286.4 5.6 %collective-permute-done.27 = f32[384,128]{1,0:T(8,128)S(1)} collective-permute-done((f32[384,128]{1,0:T(8,128)S(1)}, f32[384,128]{1,0:T(8,128)S(1)}, u32[]{:S(2)}, u32[]{:S(2)}) %collective-permute-start.27) | collective-permute-done | bytes 196640 | tf_op jit(solution)/shard_map/ppermute | solution.py:117
  293.5 2.8 convert_multiply_fusion.1
  296.3 40.4 %reduce-scatter.5.cloned.1.call-done = bf16[768,768]{1,0:T(8,128)(2,1)} async-done(((bf16[3072,768]{1,0:T(8,128)(2,1)}), bf16[768,768]{1,0:T(8,128)(2,1)}) %reduce-scatter.5.cloned.1.call-update) | async-done | bytes 1179664 | tf_op jit(solution)/shard_map/reduce_scatter | solution.py:195
  336.7 2.8 convert_multiply_fusion
  (90 shorter events, 14.6 us)
Async XLA Ops:
  7.2 236.5 %copy-start = (bf16[1,6144,128]{2,1,0:T(8,128)(2,1)S(1)}, bf16[1,6144,128]{2,1,0:T(8,128)(2,1)}, u32[]{:S(2)}) copy-start(bf16[1,6144,128]{2,1,0:T(8,128)(2,1)} %param.16) | copy-start | bytes 4718596
  7.2 286.3 %reduce-scatter.3.cloned.1.call-start = ((), (), s32[]{:S(2)}) async-start(), calls=%async_computation.2 | async-start | bytes 5898240 | tf_op jit(solution)/shard_map/reduce_scatter | solution.py:182
  7.2 29.2 %collective-permute-start.6 = (bf16[768,768]{1,0:T(8,128)(2,1)}, bf16[768,768]{1,0:T(8,128)(2,1)S(1)}, u32[]{:S(2)}, u32[]{:S(2)}) collective-permute-start(bf16[768,768]{1,0:T(8,128)(2,1)} %param.15), channel_id=1, source_target_pairs={{1,0},{2,1},{3,2},{5,4},{6,5},{7,6},{9,8},{10,9},{11,10},{13,12},{... | collective-permute-start | bytes 3538952 | tf_op jit(solution)/shard_map/ppermute | solution.py:124
  9.3 29.0 %collective-permute-start.5 = (bf16[768,768]{1,0:T(8,128)(2,1)}, bf16[768,768]{1,0:T(8,128)(2,1)}, u32[]{:S(2)}, u32[]{:S(2)}) collective-permute-start(bf16[768,768]{1,0:T(8,128)(2,1)} %param.15), channel_id=1, source_target_pairs={{0,1},{1,2},{2,3},{4,5},{5,6},{6,7},{8,9},{9,10},{10,11},{12,13},{... | collective-permute-start | bytes 3538952 | tf_op jit(solution)/shard_map/ppermute | solution.py:124
  12.7 28.2 %collective-permute-start.7 = (bf16[768,768]{1,0:T(8,128)(2,1)}, bf16[768,768]{1,0:T(8,128)(2,1)}, u32[]{:S(2)}, u32[]{:S(2)}) collective-permute-start(bf16[768,768]{1,0:T(8,128)(2,1)} %param.15), channel_id=1, source_target_pairs={{0,4},{4,0},{1,5},{5,1},{2,6},{6,2},{3,7},{7,3},{8,12},{12,8},{9,1... | collective-permute-start | bytes 3538952 | tf_op jit(solution)/shard_map/ppermute | solution.py:117
  36.4 1.9 copy-start.10
  40.8 10.0 %copy-start.3 = (s32[512]{0:T(512)S(1)}, s32[512]{0:T(512)}, u32[]{:S(2)}) copy-start(s32[512]{0:T(512)} %param.14) | copy-start | bytes 6148
  40.8 10.1 %copy-start.4 = (bf16[512,768]{1,0:T(8,128)(2,1)S(1)}, bf16[512,768]{1,0:T(8,128)(2,1)}, u32[]{:S(2)}) copy-start(bf16[512,768]{1,0:T(8,128)(2,1)} %q.3) | copy-start | bytes 2359300
  40.8 32.7 %collective-permute-start.8 = (bf16[768,768]{1,0:T(8,128)(2,1)}, bf16[768,768]{1,0:T(8,128)(2,1)}, u32[]{:S(2)}, u32[]{:S(2)}) collective-permute-start(bf16[768,768]{1,0:T(8,128)(2,1)} %collective-permute-done.5), channel_id=1, source_target_pairs={{0,1},{1,2},{2,3},{4,5},{5,6},{6,7},{8,9},{9,10},{10,11},{12,13},{... | collective-permute-start | bytes 3538952 | tf_op jit(solution)/shard_map/ppermute | solution.py:124
  44.0 29.5 %collective-permute-start.9 = (bf16[768,768]{1,0:T(8,128)(2,1)}, bf16[768,768]{1,0:T(8,128)(2,1)}, u32[]{:S(2)}, u32[]{:S(2)}) collective-permute-start(bf16[768,768]{1,0:T(8,128)(2,1)} %copy-done.10), channel_id=1, source_target_pairs={{1,0},{2,1},{3,2},{5,4},{6,5},{7,6},{9,8},{10,9},{11,10},{13,12},{... | collective-permute-start | bytes 3538952 | tf_op jit(solution)/shard_map/ppermute | solution.py:124
  49.3 17.2 %collective-permute-start = (bf16[512,768]{1,0:T(8,128)(2,1)}, bf16[512,768]{1,0:T(8,128)(2,1)}, u32[]{:S(2)}, u32[]{:S(2)}) collective-permute-start(bf16[512,768]{1,0:T(8,128)(2,1)} %constant_dynamic-slice_fusion.6), channel_id=1, source_target_pairs={{0,4},{4,0},{1,5},{5,1},{2,6},{6,2},{3,7},{7,3},{8,12},{12,8},{9,1... | collective-permute-start | bytes 2359304 | tf_op jit(solution)/shard_map/ppermute | solution.py:117
  50.4 41.4 %collective-permute-start.10 = (bf16[768,768]{1,0:T(8,128)(2,1)}, bf16[768,768]{1,0:T(8,128)(2,1)}, u32[]{:S(2)}, u32[]{:S(2)}) collective-permute-start(bf16[768,768]{1,0:T(8,128)(2,1)} %broadcast_select_fusion), channel_id=1, source_target_pairs={{0,4},{4,0},{1,5},{5,1},{2,6},{6,2},{3,7},{7,3},{8,12},{12,8},{9,1... | collective-permute-start | bytes 3538952 | tf_op jit(solution)/shard_map/ppermute | solution.py:117
  50.9 1.1 copy-start.6
  52.1 1.1 copy-start.8
  53.2 20.3 %copy-start.11 = (bf16[768,768]{1,0:T(8,128)(2,1)S(1)}, bf16[768,768]{1,0:T(8,128)(2,1)}, u32[]{:S(2)}) copy-start(bf16[768,768]{1,0:T(8,128)(2,1)} %copy-done.10) | copy-start | bytes 3538948
  59.9 14.8 %copy-start.1 = (bf16[6,512,512]{2,1,0:T(8,128)(2,1)}, bf16[6,512,512]{2,1,0:T(8,128)(2,1)S(1)}, u32[]{:S(2)}) copy-start(bf16[6,512,512]{2,1,0:T(8,128)(2,1)S(1)} %get-tuple-element.37.half) | copy-start | bytes 9437188
  60.0 48.7 %collective-permute-start.4 = (bf16[512,768]{1,0:T(8,128)(2,1)S(1)}, bf16[512,768]{1,0:T(8,128)(2,1)}, u32[]{:S(2)}, u32[]{:S(2)}) collective-permute-start(bf16[512,768]{1,0:T(8,128)(2,1)S(1)} %get-tuple-element.27), channel_id=1, source_target_pairs={{0,4},{4,0},{1,5},{5,1},{2,6},{6,2},{3,7},{7,3},{8,12},{12,8},{9,1... | collective-permute-start | bytes 2359304 | tf_op jit(solution)/shard_map/ppermute | solution.py:117
  66.6 45.2 %collective-permute-start.1 = (bf16[512,768]{1,0:T(8,128)(2,1)}, bf16[512,768]{1,0:T(8,128)(2,1)S(1)}, u32[]{:S(2)}, u32[]{:S(2)}) collective-permute-start(bf16[512,768]{1,0:T(8,128)(2,1)} %collective-permute-done), channel_id=1, source_target_pairs={{0,8},{8,16},{16,24},{24,0},{1,9},{9,17},{17,25},{25,1},{2,10},{10... | collective-permute-start | bytes 2359304 | tf_op jit(solution)/shard_map/ppermute | solution.py:117
  91.8 35.9 %collective-permute-start.11 = (bf16[768,768]{1,0:T(8,128)(2,1)}, bf16[768,768]{1,0:T(8,128)(2,1)}, u32[]{:S(2)}, u32[]{:S(2)}) collective-permute-start(bf16[768,768]{1,0:T(8,128)(2,1)} %collective-permute-done.8), channel_id=1, source_target_pairs={{0,1},{1,2},{2,3},{4,5},{5,6},{6,7},{8,9},{9,10},{10,11},{12,13},{... | collective-permute-start | bytes 3538952 | tf_op jit(solution)/shard_map/ppermute | solution.py:124
  93.8 34.0 %collective-permute-start.12 = (bf16[768,768]{1,0:T(8,128)(2,1)}, bf16[768,768]{1,0:T(8,128)(2,1)}, u32[]{:S(2)}, u32[]{:S(2)}) collective-permute-start(bf16[768,768]{1,0:T(8,128)(2,1)} %collective-permute-done.9), channel_id=1, source_target_pairs={{1,0},{2,1},{3,2},{5,4},{6,5},{7,6},{9,8},{10,9},{11,10},{13,12},{... | collective-permute-start | bytes 3538952 | tf_op jit(solution)/shard_map/ppermute | solution.py:124
  98.1 21.4 %collective-permute-start.2 = (bf16[512,768]{1,0:T(8,128)(2,1)}, bf16[512,768]{1,0:T(8,128)(2,1)}, u32[]{:S(2)}, u32[]{:S(2)}) collective-permute-start(bf16[512,768]{1,0:T(8,128)(2,1)} %collective-permute-done), channel_id=1, source_target_pairs={{0,16},{8,24},{16,0},{24,8},{1,17},{9,25},{17,1},{25,9},{2,18},{10... | collective-permute-start | bytes 2359304 | tf_op jit(solution)/shard_map/ppermute | solution.py:117
  108.7 17.8 %collective-permute-start.3 = (bf16[512,768]{1,0:T(8,128)(2,1)}, bf16[512,768]{1,0:T(8,128)(2,1)}, u32[]{:S(2)}, u32[]{:S(2)}) collective-permute-start(bf16[512,768]{1,0:T(8,128)(2,1)} %collective-permute-done), channel_id=1, source_target_pairs={{0,24},{8,0},{16,8},{24,16},{1,25},{9,1},{17,9},{25,17},{2,26},{10... | collective-permute-start | bytes 2359304 | tf_op jit(solution)/shard_map/ppermute | solution.py:117
  111.7 27.9 %collective-permute-start.13 = (bf16[768,768]{1,0:T(8,128)(2,1)}, bf16[768,768]{1,0:T(8,128)(2,1)}, u32[]{:S(2)}, u32[]{:S(2)}) collective-permute-start(bf16[768,768]{1,0:T(8,128)(2,1)} %select_select_fusion.1), channel_id=1, source_target_pairs={{0,4},{4,0},{1,5},{5,1},{2,6},{6,2},{3,7},{7,3},{8,12},{12,8},{9,1... | collective-permute-start | bytes 3538952 | tf_op jit(solution)/shard_map/ppermute | solution.py:117
  127.7 11.9 %copy-start.12 = (bf16[512,3072]{1,0:T(8,128)(2,1)S(1)}, bf16[512,3072]{1,0:T(8,128)(2,1)}, u32[]{:S(2)}) copy-start(bf16[512,3072]{1,0:T(8,128)(2,1)} %constant_dynamic-slice_fusion.7) | copy-start | bytes 9437188
  146.7 190.0 %reduce-scatter.5.cloned.1.call-start = ((), (), s32[]{:S(2)}) async-start(), calls=%async_computation.3 | async-start | bytes 5898240 | tf_op jit(solution)/shard_map/reduce_scatter | solution.py:195
  148.9 18.6 %collective-permute-start.14 = (bf16[512,768]{1,0:T(8,128)(2,1)}, bf16[512,768]{1,0:T(8,128)(2,1)}, u32[]{:S(2)}, u32[]{:S(2)}) collective-permute-start(bf16[512,768]{1,0:T(8,128)(2,1)} %constant_dynamic-slice_fusion.4), channel_id=1, source_target_pairs={{0,4},{4,0},{1,5},{5,1},{2,6},{6,2},{3,7},{7,3},{8,12},{12,8},{9,1... | collective-permute-start | bytes 2359304 | tf_op jit(solution)/shard_map/ppermute | solution.py:117
  154.5 2.7 copy-start.13
  154.6 38.2 %collective-permute-start.15 = (bf16[768,768]{1,0:T(8,128)(2,1)S(1)}, bf16[768,768]{1,0:T(8,128)(2,1)S(1)}, u32[]{:S(2)}, u32[]{:S(2)}) collective-permute-start(bf16[768,768]{1,0:T(8,128)(2,1)S(1)} %select_select_fusion), channel_id=1, source_target_pairs={{0,4},{4,0},{1,5},{5,1},{2,6},{6,2},{3,7},{7,3},{8,12},{12,8},{9,1... | collective-permute-start | bytes 3538952 | tf_op jit(solution)/shard_map/ppermute | solution.py:117
  161.5 2.4 copy-start.15
  163.9 37.8 %slice-start = ((s8[6291456]{0:T(1024)(128)(4,1)}), s8[4194304]{0:T(1024)(128)(4,1)S(1)}, s32[]{:S(2)}) async-start(s8[6291456]{0:T(1024)(128)(4,1)} %bitcast.64), calls=%async_computation.4 | async-start | bytes 8388608
  166.0 35.7 %slice-start.1 = ((s8[6291456]{0:T(1024)(128)(4,1)}), s8[2097152]{0:T(1024)(128)(4,1)S(1)}, s32[]{:S(2)}) async-start(s8[6291456]{0:T(1024)(128)(4,1)} %bitcast.64), calls=%async_computation.5 | async-start | bytes 4194304
  192.7 19.6 %collective-permute-start.16 = (bf16[512,768]{1,0:T(8,128)(2,1)}, bf16[512,768]{1,0:T(8,128)(2,1)S(1)}, u32[]{:S(2)}, u32[]{:S(2)}) collective-permute-start(bf16[512,768]{1,0:T(8,128)(2,1)} %collective-permute-done.14), channel_id=1, source_target_pairs={{0,8},{8,16},{16,24},{24,0},{1,9},{9,17},{17,25},{25,1},{2,10},{10... | collective-permute-start | bytes 2359304 | tf_op jit(solution)/shard_map/ppermute | solution.py:117
  195.2 35.1 %collective-permute-start.17 = (bf16[512,768]{1,0:T(8,128)(2,1)}, bf16[512,768]{1,0:T(8,128)(2,1)S(1)}, u32[]{:S(2)}, u32[]{:S(2)}) collective-permute-start(bf16[512,768]{1,0:T(8,128)(2,1)} %collective-permute-done.14), channel_id=1, source_target_pairs={{0,16},{8,24},{16,0},{24,8},{1,17},{9,25},{17,1},{25,9},{2,18},{10... | collective-permute-start | bytes 2359304 | tf_op jit(solution)/shard_map/ppermute | solution.py:117
  195.7 35.3 %collective-permute-start.18 = (bf16[512,768]{1,0:T(8,128)(2,1)}, bf16[512,768]{1,0:T(8,128)(2,1)S(1)}, u32[]{:S(2)}, u32[]{:S(2)}) collective-permute-start(bf16[512,768]{1,0:T(8,128)(2,1)} %collective-permute-done.14), channel_id=1, source_target_pairs={{0,24},{8,0},{16,8},{24,16},{1,25},{9,1},{17,9},{25,17},{2,26},{10... | collective-permute-start | bytes 2359304 | tf_op jit(solution)/shard_map/ppermute | solution.py:117
  195.7 2.3 copy-start.2
  200.4 30.6 %collective-permute-start.19 = (bf16[512,768]{1,0:T(8,128)(2,1)S(1)}, bf16[512,768]{1,0:T(8,128)(2,1)S(1)}, u32[]{:S(2)}, u32[]{:S(2)}) collective-permute-start(bf16[512,768]{1,0:T(8,128)(2,1)S(1)} %value_grad.1), channel_id=1, source_target_pairs={{0,4},{4,0},{1,5},{5,1},{2,6},{6,2},{3,7},{7,3},{8,12},{12,8},{9,1... | collective-permute-start | bytes 2359304 | tf_op jit(solution)/shard_map/ppermute | solution.py:117
  238.2 2.6 copy-start.14
  241.8 11.9 %collective-permute-start.20 = (bf16[512,128]{1,0:T(8,128)(2,1)S(1)}, bf16[512,128]{1,0:T(8,128)(2,1)}, u32[]{:S(2)}, u32[]{:S(2)}) collective-permute-start(bf16[512,128]{1,0:T(8,128)(2,1)S(1)} %get-tuple-element.60), channel_id=1, source_target_pairs={{0,8},{8,16},{16,24},{24,0},{1,9},{9,17},{17,25},{25,1},{2,10},{10... | collective-permute-start | bytes 393224 | tf_op jit(solution)/shard_map/ppermute | solution.py:117
  241.9 11.9 %collective-permute-start.21 = (bf16[512,128]{1,0:T(8,128)(2,1)S(1)}, bf16[512,128]{1,0:T(8,128)(2,1)}, u32[]{:S(2)}, u32[]{:S(2)}) collective-permute-start(bf16[512,128]{1,0:T(8,128)(2,1)S(1)} %get-tuple-element.60), channel_id=1, source_target_pairs={{0,16},{8,24},{16,0},{24,8},{1,17},{9,25},{17,1},{25,9},{2,18},{10... | collective-permute-start | bytes 393224 | tf_op jit(solution)/shard_map/ppermute | solution.py:117
  242.9 10.9 %collective-permute-start.22 = (bf16[512,128]{1,0:T(8,128)(2,1)S(1)}, bf16[512,128]{1,0:T(8,128)(2,1)}, u32[]{:S(2)}, u32[]{:S(2)}) collective-permute-start(bf16[512,128]{1,0:T(8,128)(2,1)S(1)} %get-tuple-element.60), channel_id=1, source_target_pairs={{0,24},{8,0},{16,8},{24,16},{1,25},{9,1},{17,9},{25,17},{2,26},{10... | collective-permute-start | bytes 393224 | tf_op jit(solution)/shard_map/ppermute | solution.py:117
  251.3 31.5 %collective-permute-start.29 = (bf16[32,768]{1,0:T(8,128)(2,1)S(1)}, bf16[32,768]{1,0:T(8,128)(2,1)S(1)}, u32[]{:S(2)}, u32[]{:S(2)}) collective-permute-start(bf16[32,768]{1,0:T(8,128)(2,1)S(1)} %get-tuple-element.57), channel_id=1, source_target_pairs={{0,1},{1,2},{2,3},{3,0},{4,5},{5,6},{6,7},{7,4},{8,9},{9,10},{10,1... | collective-permute-start | bytes 147464 | tf_op jit(solution)/shard_map/ppermute | solution.py:117
  251.3 31.4 %collective-permute-start.30 = (bf16[32,768]{1,0:T(8,128)(2,1)S(1)}, bf16[32,768]{1,0:T(8,128)(2,1)S(1)}, u32[]{:S(2)}, u32[]{:S(2)}) collective-permute-start(bf16[32,768]{1,0:T(8,128)(2,1)S(1)} %get-tuple-element.59), channel_id=1, source_target_pairs={{0,2},{1,3},{2,0},{3,1},{4,6},{5,7},{6,4},{7,5},{8,10},{9,11},{10,... | collective-permute-start | bytes 147464 | tf_op jit(solution)/shard_map/ppermute | solution.py:117
  253.8 5.9 %copy-start.5 = (bf16[512,768]{1,0:T(8,128)(2,1)S(1)}, bf16[512,768]{1,0:T(8,128)(2,1)}, u32[]{:S(2)}) copy-start(bf16[512,768]{1,0:T(8,128)(2,1)} %q.3) | copy-start | bytes 2359300
  253.8 5.9 %copy-start.7 = (bf16[512,768]{1,0:T(8,128)(2,1)S(1)}, bf16[512,768]{1,0:T(8,128)(2,1)}, u32[]{:S(2)}) copy-start(bf16[512,768]{1,0:T(8,128)(2,1)} %k.3) | copy-start | bytes 2359300
  253.8 5.9 %copy-start.9 = (bf16[512,768]{1,0:T(8,128)(2,1)S(1)}, bf16[512,768]{1,0:T(8,128)(2,1)}, u32[]{:S(2)}) copy-start(bf16[512,768]{1,0:T(8,128)(2,1)} %v.3) | copy-start | bytes 2359300
  256.2 11.6 %collective-permute-start.23 = (bf16[384,128]{1,0:T(8,128)(2,1)S(1)}, bf16[384,128]{1,0:T(8,128)(2,1)S(1)}, u32[]{:S(2)}, u32[]{:S(2)}) collective-permute-start(bf16[384,128]{1,0:T(8,128)(2,1)S(1)} %get-tuple-element.54), channel_id=1, source_target_pairs={{0,1},{1,2},{2,3},{3,0},{4,5},{5,6},{6,7},{7,4},{8,9},{9,10},{10,1... | collective-permute-start | bytes 294920 | tf_op jit(solution)/shard_map/ppermute | solution.py:117
  256.4 20.4 %collective-permute-start.24 = (bf16[384,128]{1,0:T(8,128)(2,1)S(1)}, bf16[384,128]{1,0:T(8,128)(2,1)S(1)}, u32[]{:S(2)}, u32[]{:S(2)}) collective-permute-start(bf16[384,128]{1,0:T(8,128)(2,1)S(1)} %get-tuple-element.56), channel_id=1, source_target_pairs={{0,2},{1,3},{2,0},{3,1},{4,6},{5,7},{6,4},{7,5},{8,10},{9,11},{10,... | collective-permute-start | bytes 294920 | tf_op jit(solution)/shard_map/ppermute | solution.py:117
  259.7 21.1 %collective-permute-start.25 = (bf16[384,128]{1,0:T(8,128)(2,1)S(1)}, bf16[384,128]{1,0:T(8,128)(2,1)S(1)}, u32[]{:S(2)}, u32[]{:S(2)}) collective-permute-start(bf16[384,128]{1,0:T(8,128)(2,1)S(1)} %get-tuple-element.55), channel_id=1, source_target_pairs={{0,3},{1,0},{2,1},{3,2},{4,7},{5,4},{6,5},{7,6},{8,11},{9,8},{10,9... | collective-permute-start | bytes 294920 | tf_op jit(solution)/shard_map/ppermute | solution.py:117
  267.9 15.3 %collective-permute-start.31 = (bf16[32,768]{1,0:T(8,128)(2,1)S(1)}, bf16[32,768]{1,0:T(8,128)(2,1)S(1)}, u32[]{:S(2)}, u32[]{:S(2)}) collective-permute-start(bf16[32,768]{1,0:T(8,128)(2,1)S(1)} %get-tuple-element.58), channel_id=1, source_target_pairs={{0,3},{1,0},{2,1},{3,2},{4,7},{5,4},{6,5},{7,6},{8,11},{9,8},{10,9... | collective-permute-start | bytes 147464 | tf_op jit(solution)/shard_map/ppermute | solution.py:117
  280.9 5.4 %collective-permute-start.26 = (f32[384,128]{1,0:T(8,128)S(1)}, f32[384,128]{1,0:T(8,128)S(1)}, u32[]{:S(2)}, u32[]{:S(2)}) collective-permute-start(f32[384,128]{1,0:T(8,128)S(1)} %get-tuple-element.49), channel_id=1, source_target_pairs={{0,8},{8,16},{16,24},{24,0},{1,9},{9,17},{17,25},{25,1},{2,10},{10... | collective-permute-start | bytes 589832 | tf_op jit(solution)/shard_map/ppermute | solution.py:117
  282.2 9.7 %collective-permute-start.27 = (f32[384,128]{1,0:T(8,128)S(1)}, f32[384,128]{1,0:T(8,128)S(1)}, u32[]{:S(2)}, u32[]{:S(2)}) collective-permute-start(f32[384,128]{1,0:T(8,128)S(1)} %get-tuple-element.49), channel_id=1, source_target_pairs={{0,16},{8,24},{16,0},{24,8},{1,17},{9,25},{17,1},{25,9},{2,18},{10... | collective-permute-start | bytes 589832 | tf_op jit(solution)/shard_map/ppermute | solution.py:117
  284.7 7.9 %collective-permute-start.28 = (f32[384,128]{1,0:T(8,128)S(1)}, f32[384,128]{1,0:T(8,128)S(1)}, u32[]{:S(2)}, u32[]{:S(2)}) collective-permute-start(f32[384,128]{1,0:T(8,128)S(1)} %get-tuple-element.49), channel_id=1, source_target_pairs={{0,24},{8,0},{16,8},{24,16},{1,25},{9,1},{17,9},{25,17},{2,26},{10... | collective-permute-start | bytes 589832 | tf_op jit(solution)/shard_map/ppermute | solution.py:117
Sparse Core Ops, SparseCore 0:
  146.9 86.4 reduce-scatter.2
  238.2 98.4 reduce-scatter.4
